TPU v7x, 32 devices: a whole 2x2x4 slice. The times are simulated.
32 devices in a mesh: sec: 8 (over z, x), blk: 4 (over y, core).
Axes of the slice: x: 2, y: 2, z: 4, core: 2. Of those that a mesh axis runs over, the one named last changes fastest.
Arguments:
- features: bfloat16 [8, 52, 8192], P('sec', None, 'blk'), may hold values from -6 to 6
- programs: bfloat16 [8, 32, 8192], P('sec', None, 'blk'), may hold values from -6 to 6
- column_pot: bfloat16 [8, 8192], P('sec', 'blk'), may hold values from -12 to 12
- tile_pairs: int32 [2, 8, 112], P(None, 'sec', 'blk'), may hold values from 0 to 15, as said below
- pair_counts: int32 [8, 4], P('sec', 'blk'), may hold values from 0 to 28, as said below
Outputs:
- smoothed: bfloat16 [8, 32, 8192], P('sec', None, 'blk')
- row_potential: float32 [8, 8192], P('sec', 'blk')
- column_potential: float32 [8, 8192], P('sec', 'blk')
Inputs may be any that keep to these rules, and one draw needn't show every extreme that they name: `tile_pairs`: entry [0, s, b * 28 + k] is a row tile of block b of section s counted within the block (0 to 3); entry [1, s, b * 28 + k] is a tile of section s + 1 (0 to 15). Only slots k < pair_counts[s, b] are active; slots from there on hold in-range entries that do not count. The active pairs of one block are distinct; in every section but the last, every row tile of every block is in an active pair, and every tile of section s + 1 is in an active pair of section s. `pair_counts`: 0 in the last section; in every other section from 4 to 28, and one block of every such section holds exactly 28.
All inputs are finite; a program needn't handle non-finite values.
Results may differ from a plain program's by a relative error of at most 0.0034.
Values may be sent and summed in bfloat16 or wider, within the bound.
A program may use at most 64 MiB of HBM per device.

v0:
```python
import jax
import jax.numpy as jnp
from jax import lax
from jax.sharding import PartitionSpec as P

FEAT = 52
TILE = 512


EPSILON = 0.05
NEG_FILL = -1e30


def passed_along(value, axis, steps):
    count = lax.axis_size(axis)
    initial, last = (max(0, -steps), min(count, count - steps))
    return lax.ppermute(value, axis, [(source, source + steps) for source in range(initial, last)])


def merged(part, axis, combine):
    gathered = jax.tree.map(lambda a: lax.all_gather(a, axis), part)

    def take(source):
        return jax.tree.map(lambda a: lax.dynamic_index_in_dim(a, source, 0, False), gathered)

    return lax.fori_loop(
        1, lax.axis_size(axis), lambda source, state: combine(state, take(source)), take(0)
    )


def merge_lse(first_lse, second_lse):
    highest = jnp.maximum(first_lse[0], second_lse[0])
    return (
        highest,
        first_lse[1] * jnp.exp(first_lse[0] - highest)
        + second_lse[1] * jnp.exp(second_lse[0] - highest),
    )


def tile_cost(row_x, row_sq, col_x, col_sq, row_tile, col_tile):
    row_block = lax.dynamic_slice_in_dim(row_x, row_tile * TILE, TILE, 1)
    col_block = lax.dynamic_slice_in_dim(col_x, col_tile * TILE, TILE, 1)
    inner = lax.dot_general(
        row_block, col_block, (((0,), (0,)), ((), ())), preferred_element_type=jnp.float32
    )
    row_part = lax.dynamic_slice_in_dim(row_sq, row_tile * TILE, TILE, 0)
    col_part = lax.dynamic_slice_in_dim(col_sq, col_tile * TILE, TILE, 0)
    return (row_part[:, None] + col_part[None, :] - 2.0 * inner) / FEAT


def fold_lse(carry_lse, scores, offset, reduce_axis):
    tile_max = jnp.max(scores, axis=reduce_axis)
    tile_sum = jnp.sum(jnp.exp(scores - jnp.expand_dims(tile_max, reduce_axis)), axis=reduce_axis)
    old_max = lax.dynamic_slice_in_dim(carry_lse[0], offset, TILE, 0)
    old_sum = lax.dynamic_slice_in_dim(carry_lse[1], offset, TILE, 0)
    new_max, new_sum = merge_lse((old_max, old_sum), (tile_max, tile_sum))
    return (
        lax.dynamic_update_slice_in_dim(carry_lse[0], new_max, offset, 0),
        lax.dynamic_update_slice_in_dim(carry_lse[1], new_sum, offset, 0),
    )


def body(features, programs, column_pot, tile_pairs, pair_counts):
    cells_blk = features.shape[2]
    tiles_blk = cells_blk // TILE
    most_pairs = tile_pairs.shape[2]
    blocks = lax.axis_size("blk")
    block = lax.axis_index("blk")
    at_end = lax.axis_index("sec") == lax.axis_size("sec") - 1
    whole_x, whole_prog, whole_pot = (
        lax.all_gather(features, "blk", axis=2, tiled=True),
        lax.all_gather(programs, "blk", axis=2, tiled=True),
        lax.all_gather(column_pot, "blk", axis=1, tiled=True),
    )
    next_x, next_prog = passed_along((whole_x, whole_prog), "sec", -1)
    col_x = next_x[0]
    all_cells = col_x.shape[1]
    col_ext = jnp.concatenate([next_prog[0], jnp.ones((1, all_cells), jnp.bfloat16)], axis=0)
    pot_in = whole_pot[0].astype(jnp.float32)
    all_x, all_prog = (
        lax.all_gather(features, "blk", axis=2, tiled=True),
        lax.all_gather(programs, "blk", axis=2, tiled=True),
    )
    all_pairs, all_counts = (
        lax.all_gather(tile_pairs, "blk", axis=2, tiled=True),
        lax.all_gather(pair_counts, "blk", axis=1, tiled=True),
    )
    row_x = all_x[0]
    row_ext = jnp.concatenate([all_prog[0], jnp.ones((1, all_cells), jnp.bfloat16)], axis=0)
    counts = all_counts[0]
    ends_at = jnp.cumsum(counts)
    starts_at = ends_at - counts
    total_pairs = jnp.sum(counts)
    share_size = (total_pairs + blocks - 1) // blocks
    first_item = jnp.minimum(block * share_size, total_pairs)
    n_items = jnp.minimum(total_pairs - first_item, share_size)
    block_ids = jnp.arange(blocks, dtype=jnp.int32)

    def item_of(item):
        rank_global = first_item + item
        owner_blk = jnp.sum((ends_at <= rank_global).astype(jnp.int32))
        first_rank = jnp.sum(jnp.where(block_ids == owner_blk, starts_at, 0))
        slot_index = owner_blk * most_pairs + rank_global - first_rank
        return (all_pairs[0, 0, slot_index] + owner_blk * tiles_blk, all_pairs[1, 0, slot_index])

    rows_here = row_x.shape[1]
    row_sq = jnp.sum(jnp.square(row_x.astype(jnp.float32)), axis=0)
    col_sq = jnp.sum(jnp.square(col_x.astype(jnp.float32)), axis=0)

    def row_fold(item, carry_lse):
        row_tile, col_tile = item_of(item)
        cost = tile_cost(row_x, row_sq, col_x, col_sq, row_tile, col_tile)
        column = lax.dynamic_slice_in_dim(pot_in, col_tile * TILE, TILE, 0)
        scores = (column[None, :] - cost) / EPSILON
        return fold_lse(carry_lse, scores, row_tile * TILE, 1)

    row_empty = (
        jnp.full((rows_here,), NEG_FILL, jnp.float32),
        jnp.zeros((rows_here,), jnp.float32),
    )
    row_lse = lax.fori_loop(0, n_items, row_fold, row_empty)
    row_lse = merged(row_lse, "blk", merge_lse)
    row_pot = jnp.where(at_end, 0.0, -EPSILON * (row_lse[0] + jnp.log(row_lse[1])))

    def col_fold(item, carry_lse):
        row_tile, col_tile = item_of(item)
        cost = tile_cost(row_x, row_sq, col_x, col_sq, row_tile, col_tile)
        row_part = lax.dynamic_slice_in_dim(row_pot, row_tile * TILE, TILE, 0)
        scores = (row_part[:, None] - cost) / EPSILON
        return fold_lse(carry_lse, scores, col_tile * TILE, 0)

    col_empty = (
        jnp.full((all_cells,), NEG_FILL, jnp.float32),
        jnp.zeros((all_cells,), jnp.float32),
    )
    col_lse = lax.fori_loop(0, n_items, col_fold, col_empty)
    col_lse = merged(col_lse, "blk", merge_lse)
    col_new = jnp.where(at_end, 0.0, -EPSILON * (col_lse[0] + jnp.log(col_lse[1])))

    def plan_fold(item, sums):
        row_num, col_num = sums
        row_tile, col_tile = item_of(item)
        cost = tile_cost(row_x, row_sq, col_x, col_sq, row_tile, col_tile)
        row_part = lax.dynamic_slice_in_dim(row_pot, row_tile * TILE, TILE, 0)
        col_part = lax.dynamic_slice_in_dim(col_new, col_tile * TILE, TILE, 0)
        plan = jnp.exp((row_part[:, None] + col_part[None, :] - cost) / EPSILON).astype(
            jnp.bfloat16
        )
        col_prog = lax.dynamic_slice_in_dim(col_ext, col_tile * TILE, TILE, 1)
        row_prog = lax.dynamic_slice_in_dim(row_ext, row_tile * TILE, TILE, 1)
        to_rows = lax.dot_general(
            col_prog, plan, (((1,), (1,)), ((), ())), preferred_element_type=jnp.float32
        )
        to_cols = lax.dot_general(
            row_prog, plan, (((1,), (0,)), ((), ())), preferred_element_type=jnp.float32
        )
        old_rows = lax.dynamic_slice_in_dim(row_num, row_tile * TILE, TILE, 1)
        old_cols = lax.dynamic_slice_in_dim(col_num, col_tile * TILE, TILE, 1)
        row_num = lax.dynamic_update_slice_in_dim(row_num, old_rows + to_rows, row_tile * TILE, 1)
        col_num = lax.dynamic_update_slice_in_dim(col_num, old_cols + to_cols, col_tile * TILE, 1)
        return (row_num, col_num)

    width_ext = col_ext.shape[0]
    start_sums = (
        jnp.zeros((width_ext, rows_here), jnp.float32),
        jnp.zeros((width_ext, all_cells), jnp.float32),
    )
    row_num, col_num = lax.fori_loop(0, n_items, plan_fold, start_sums)
    moved = passed_along(col_num, "sec", 1)
    arrived = lax.psum_scatter(moved, "blk", scatter_dimension=1, tiled=True)
    row_num = lax.psum_scatter(row_num, "blk", scatter_dimension=1, tiled=True)
    own_row_pot = lax.dynamic_slice_in_dim(row_pot, block * cells_blk, cells_blk, 0)
    own_col_pot = lax.dynamic_slice_in_dim(col_new, block * cells_blk, cells_blk, 0)
    totals = row_num + arrived
    progs_count = width_ext - 1
    smoothed = (totals[:progs_count] / totals[progs_count:]).astype(jnp.bfloat16)
    return (smoothed[None], own_row_pot[None], own_col_pot[None])


def solution(mesh):
    in_specs = (
        P("sec", None, "blk"),
        P("sec", None, "blk"),
        P("sec", "blk"),
        P(None, "sec", "blk"),
        P("sec", "blk"),
    )
    out_specs = (P("sec", None, "blk"), P("sec", "blk"), P("sec", "blk"))
    return jax.shard_map(body, mesh=mesh, in_specs=in_specs, out_specs=out_specs, check_vma=False)
```

profile of v0, /device:TPU:0, one launch (start us, length us, event | category | flops | bytes accessed | tf_op | source)
XLA Modules:
  0.0 436.6 jit_solution(18211607701423082297)
XLA Ops:
  7.2 11.0 %all_gather.45 = bf16[1,52,8192]{2,1,0:T(8,128)(2,1)S(1)} all-gather(bf16[1,52,2048]{2,1,0:T(8,128)(2,1)} %param.15), channel_id=1, replica_groups=mesh['sec'=8,'blk'=4] {'blk'}, dimensions={2}, use_global_device_ids=true | all-gather | bytes 1064960 | tf_op jit(solution)/shard_map/all_gather | solution.py:81
  18.3 1.3 collective-permute-start.1
  19.6 7.5 %all_gather.43 = bf16[1,32,8192]{2,1,0:T(8,128)(2,1)S(1)} all-gather(bf16[1,32,2048]{2,1,0:T(8,128)(2,1)} %param.16), channel_id=1, replica_groups=mesh['sec'=8,'blk'=4] {'blk'}, dimensions={2}, use_global_device_ids=true | all-gather | bytes 655360 | tf_op jit(solution)/shard_map/all_gather | solution.py:72
  27.1 1.3 collective-permute-start
  30.3 4.5 %all-reduce.2 = s32[4]{0:T(128)S(1)} all-reduce(s32[4]{0:T(128)S(1)} %bitcast_dynamic-update-slice_fusion), channel_id=1, replica_groups=mesh['sec'=8,'blk'=4] {'blk'}, use_global_device_ids=true, to_apply=%add.2 | all-reduce | flops 4 | bytes 32 | tf_op jit(solution)/shard_map/squeeze | solution.py:90
  37.7 5.2 %all_gather.42 = s32[2,1,112]{0,1,2:T(1,128)S(1)} all-gather(s32[2,1,28]{0,1,2:T(1,128)S(1)} %copy.8), channel_id=1, replica_groups=mesh['sec'=8,'blk'=4] {'blk'}, dimensions={2}, use_global_device_ids=true | all-gather | bytes 1120 | tf_op jit(solution)/shard_map/all_gather | solution.py:85
  43.0 5.2 %all_gather.44 = bf16[1,8192]{1,0:T(2,128)(2,1)S(1)} all-gather(bf16[1,2048]{1,0:T(2,128)(2,1)S(1)} %copy-done.4), channel_id=1, replica_groups=mesh['sec'=8,'blk'=4] {'blk'}, dimensions={1}, use_global_device_ids=true | all-gather | bytes 20480 | tf_op jit(solution)/shard_map/all_gather | solution.py:73
  49.4 4.6 %collective-permute-done = bf16[1,32,8192]{2,1,0:T(8,128)(2,1)S(1)} collective-permute-done((bf16[1,32,8192]{2,1,0:T(8,128)(2,1)S(1)}, bf16[1,32,8192]{2,1,0:T(8,128)(2,1)S(1)}, u32[]{:S(2)}, u32[]{:S(2)}) %collective-permute-start) | collective-permute-done | bytes 524320 | tf_op jit(solution)/shard_map/ppermute | solution.py:17
  55.2 71.8 %while.75 = (s32[]{:T(128)}, f32[8192]{0:T(1024)S(1)}, f32[8192]{0:T(1024)S(1)}, s32[]{:T(128)}, s32[]{:T(128)}, /*index=5*/s32[4]{0:T(128)S(1)}, s32[4]{0:T(128...) while((s32[]{:T(128)}, f32[8192]{0:T(1024)S(1)}, ...), condition=%wide.region_9.10_spmd.clone, body=%wide.region_4.9_spmd.clone.sunk | while | flops 29624360 | bytes 2249183 | solution.py:121
  56.6 1.4 fusion.65
  63.8 1.4 fusion.65
  70.9 1.4 fusion.65
  78.1 1.4 fusion.65
  85.3 1.4 fusion.65
  92.5 1.4 fusion.65
  99.7 1.4 fusion.65
  106.8 1.4 fusion.65
  114.0 1.4 fusion.65
  121.2 1.4 fusion.65
  127.0 5.4 %all-gather = f32[32768]{0:T(1024)S(1)} all-gather(f32[8192]{0:T(1024)S(1)} %get-tuple-element.506), channel_id=2, replica_groups=mesh['sec'=8,'blk'=4] {'blk'}, dimensions={0}, use_global_device_ids=true | all-gather | bytes 163840 | tf_op jit(solution)/shard_map/all_gather | solution.py:21
  132.5 5.4 %all-gather.1 = f32[32768]{0:T(1024)S(1)} all-gather(f32[8192]{0:T(1024)S(1)} %get-tuple-element.507), channel_id=3, replica_groups=mesh['sec'=8,'blk'=4] {'blk'}, dimensions={0}, use_global_device_ids=true | all-gather | bytes 163840 | tf_op jit(solution)/shard_map/all_gather | solution.py:21
  138.4 67.7 %while.76 = (s32[]{:T(128)}, f32[8192]{0:T(1024)S(1)}, f32[8192]{0:T(1024)S(1)}, s32[]{:T(128)}, s32[]{:T(128)}, /*index=5*/s32[4]{0:T(128)S(1)}, s32[4]{0:T(128...) while((s32[]{:T(128)}, f32[8192]{0:T(1024)S(1)}, ...), condition=%wide.region_17.18_spmd.clone, body=%wide.region_12.17_spmd.clone.sunk | while | flops 29624360 | bytes 2249183 | solution.py:136
  139.6 1.2 fusion.68
  146.4 1.2 fusion.68
  153.1 1.2 fusion.68
  159.9 1.2 fusion.68
  166.7 1.2 fusion.68
  173.4 1.2 fusion.68
  180.2 1.2 fusion.68
  187.0 1.2 fusion.68
  193.7 1.2 fusion.68
  200.5 1.2 fusion.68
  206.7 5.4 %all-gather.2 = f32[32768]{0:T(1024)S(1)} all-gather(f32[8192]{0:T(1024)S(1)} %get-tuple-element.510), channel_id=4, replica_groups=mesh['sec'=8,'blk'=4] {'blk'}, dimensions={0}, use_global_device_ids=true | all-gather | bytes 163840 | tf_op jit(solution)/shard_map/all_gather | solution.py:21
  212.2 5.4 %all-gather.3 = f32[32768]{0:T(1024)S(1)} all-gather(f32[8192]{0:T(1024)S(1)} %get-tuple-element.511), channel_id=5, replica_groups=mesh['sec'=8,'blk'=4] {'blk'}, dimensions={0}, use_global_device_ids=true | all-gather | bytes 163840 | tf_op jit(solution)/shard_map/all_gather | solution.py:21
  218.9 120.7 %while.77 = (s32[]{:T(128)}, f32[33,8192]{1,0:T(8,128)S(1)}, f32[33,8192]{1,0:T(8,128)S(1)}, s32[]{:T(128)}, s32[]{:T(128)}, /*index=5*/s32[4]{0:T(128)S(1)}, s3...) while((s32[]{:T(128)}, f32[33,8192]{1,0:T(8,128)S(1)}, ...), condition=%wide.region_23.24_spmd.clone, body=%wide.region_20.23_spmd.clone.sunk | while | flops 63996968 | bytes 2122431 | solution.py:168
  220.1 1.2 fusion.77
  227.5 1.3 fusion.78
  229.9 1.1 fusion.79
  232.2 1.2 fusion.77
  239.6 1.3 fusion.78
  244.3 1.2 fusion.77
  251.7 1.3 fusion.78
  256.3 1.2 fusion.77
  263.8 1.3 fusion.78
  268.4 1.2 fusion.77
  275.8 1.3 fusion.78
  280.5 1.2 fusion.77
  287.9 1.3 fusion.78
  292.6 1.2 fusion.77
  300.0 1.3 fusion.78
  304.6 1.2 fusion.77
  312.0 1.3 fusion.78
  316.7 1.2 fusion.77
  324.1 1.3 fusion.78
  326.5 1.1 fusion.79
  328.8 1.2 fusion.77
  336.2 1.3 fusion.78
  339.6 30.3 %collective-permute-start.2 = (f32[33,8192]{1,0:T(8,128)S(1)}, f32[33,8192]{1,0:T(8,128)S(1)}, u32[]{:S(2)}, u32[]{:S(2)}) collective-permute-start(f32[33,8192]{1,0:T(8,128)S(1)} %get-tuple-element.515), channel_id=1, source_target_pairs={{0,4},{4,8},{8,12},{12,16},{16,20},{20,24},{24,28},{1,5},{5,9},{9,... | collective-permute-start | bytes 3244040 | tf_op jit(solution)/shard_map/ppermute | solution.py:17
  370.0 28.4 %collective-permute-done.2 = f32[33,8192]{1,0:T(8,128)S(1)} collective-permute-done((f32[33,8192]{1,0:T(8,128)S(1)}, f32[33,8192]{1,0:T(8,128)S(1)}, u32[]{:S(2)}, u32[]{:S(2)}) %collective-permute-start.2) | collective-permute-done | bytes 1081376 | tf_op jit(solution)/shard_map/ppermute | solution.py:17
  398.4 1.2 add.277
  399.7 1.3 dynamic_slice.154
  401.0 1.3 dynamic_slice.153
  402.3 25.0 %reduce-scatter.2.cloned.1.call-done = f32[33,2048]{1,0:T(8,128)} async-done(((f32[33,8192]{1,0:T(8,128)}), f32[33,2048]{1,0:T(8,128)}) %reduce-scatter.2.cloned.1.call-update) | async-done | bytes 270352 | tf_op jit(solution)/shard_map/reduce_scatter | solution.py:171
  428.1 1.6 fusion.42
  (338 shorter events, 118.4 us)
Async XLA Ops:
  7.2 21.8 %copy-start.8 = (u32[32]{0:T(128)S(1)}, u32[32]{0:T(128)}, u32[]{:S(2)}) copy-start(u32[32]{0:T(128)} %constant.224) | copy-start | bytes 388
  7.2 30.4 %copy-start.5 = (s32[2,1,28]{2,1,0:T(1,128)S(1)}, s32[2,1,28]{2,1,0:T(1,128)}, u32[]{:S(2)}) copy-start(s32[2,1,28]{2,1,0:T(1,128)} %param.18) | copy-start | bytes 676
  7.2 35.8 %copy-start.4 = (bf16[1,2048]{1,0:T(2,128)(2,1)S(1)}, bf16[1,2048]{1,0:T(2,128)(2,1)}, u32[]{:S(2)}) copy-start(bf16[1,2048]{1,0:T(2,128)(2,1)} %param.17) | copy-start | bytes 12292
  7.2 420.1 %reduce-scatter.2.cloned.1.call-start = ((), (), s32[]{:S(2)}) async-start(), calls=%async_computation.1 | async-start | bytes 1638400 | tf_op jit(solution)/shard_map/reduce_scatter | solution.py:171
  18.3 36.6 %collective-permute-start.1 = (bf16[1,52,8192]{2,1,0:T(8,128)(2,1)S(1)}, bf16[1,52,8192]{2,1,0:T(8,128)(2,1)S(1)}, u32[]{:S(2)}, u32[]{:S(2)}) collective-permute-start(bf16[1,52,8192]{2,1,0:T(8,128)(2,1)S(1)} %all_gather.45), channel_id=1, source_target_pairs={{4,0},{8,4},{12,8},{16,12},{20,16},{24,20},{28,24},{5,1},{9,5},{13... | collective-permute-start | bytes 2555912 | tf_op jit(solution)/shard_map/ppermute | solution.py:17
  27.1 26.9 %collective-permute-start = (bf16[1,32,8192]{2,1,0:T(8,128)(2,1)S(1)}, bf16[1,32,8192]{2,1,0:T(8,128)(2,1)S(1)}, u32[]{:S(2)}, u32[]{:S(2)}) collective-permute-start(bf16[1,32,8192]{2,1,0:T(8,128)(2,1)S(1)} %all_gather.43), channel_id=1, source_target_pairs={{4,0},{8,4},{12,8},{16,12},{20,16},{24,20},{28,24},{5,1},{9,5},{13... | collective-permute-start | bytes 1572872 | tf_op jit(solution)/shard_map/ppermute | solution.py:17
  206.1 0.6 copy-start.3
  206.7 11.0 %copy-start = (bf16[52,8192]{1,0:T(8,128)(2,1)}, bf16[52,8192]{1,0:T(8,128)(2,1)S(1)}, u32[]{:S(2)}) copy-start(bf16[52,8192]{1,0:T(8,128)(2,1)S(1)} %get-tuple-element.1400) | copy-start | bytes 2555908
  206.7 11.0 %copy-start.1 = (f32[8192]{0:T(1024)}, f32[8192]{0:T(1024)S(1)}, u32[]{:S(2)}) copy-start(f32[8192]{0:T(1024)S(1)} %get-tuple-element.1406) | copy-start | bytes 98308
  206.7 11.0 %copy-start.2 = (f32[8192]{0:T(1024)}, f32[8192]{0:T(1024)S(1)}, u32[]{:S(2)}) copy-start(f32[8192]{0:T(1024)S(1)} %get-tuple-element.1408) | copy-start | bytes 98308
  218.9 4.4 %copy-start.6 = (s32[4]{0:T(128)}, s32[4]{0:T(128)S(1)}, u32[]{:S(2)}) copy-start(s32[4]{0:T(128)S(1)} %get-tuple-element.1371) | copy-start | bytes 52 | tf_op jit(solution)/shard_map/while
  228.9 2.1 copy-start.7
  231.0 4.4 %copy-start.6 = (s32[4]{0:T(128)}, s32[4]{0:T(128)S(1)}, u32[]{:S(2)}) copy-start(s32[4]{0:T(128)S(1)} %get-tuple-element.1371) | copy-start | bytes 52 | tf_op jit(solution)/shard_map/while
  241.0 2.1 copy-start.7
  243.1 4.4 %copy-start.6 = (s32[4]{0:T(128)}, s32[4]{0:T(128)S(1)}, u32[]{:S(2)}) copy-start(s32[4]{0:T(128)S(1)} %get-tuple-element.1371) | copy-start | bytes 52 | tf_op jit(solution)/shard_map/while
  253.0 2.1 copy-start.7
  255.1 4.4 %copy-start.6 = (s32[4]{0:T(128)}, s32[4]{0:T(128)S(1)}, u32[]{:S(2)}) copy-start(s32[4]{0:T(128)S(1)} %get-tuple-element.1371) | copy-start | bytes 52 | tf_op jit(solution)/shard_map/while
  265.1 2.1 copy-start.7
  267.2 4.4 %copy-start.6 = (s32[4]{0:T(128)}, s32[4]{0:T(128)S(1)}, u32[]{:S(2)}) copy-start(s32[4]{0:T(128)S(1)} %get-tuple-element.1371) | copy-start | bytes 52 | tf_op jit(solution)/shard_map/while
  277.2 2.1 copy-start.7
  279.3 4.4 %copy-start.6 = (s32[4]{0:T(128)}, s32[4]{0:T(128)S(1)}, u32[]{:S(2)}) copy-start(s32[4]{0:T(128)S(1)} %get-tuple-element.1371) | copy-start | bytes 52 | tf_op jit(solution)/shard_map/while
  289.2 2.1 copy-start.7
  291.3 4.4 %copy-start.6 = (s32[4]{0:T(128)}, s32[4]{0:T(128)S(1)}, u32[]{:S(2)}) copy-start(s32[4]{0:T(128)S(1)} %get-tuple-element.1371) | copy-start | bytes 52 | tf_op jit(solution)/shard_map/while
  301.3 2.1 copy-start.7
  303.4 4.4 %copy-start.6 = (s32[4]{0:T(128)}, s32[4]{0:T(128)S(1)}, u32[]{:S(2)}) copy-start(s32[4]{0:T(128)S(1)} %get-tuple-element.1371) | copy-start | bytes 52 | tf_op jit(solution)/shard_map/while
  313.4 2.1 copy-start.7
  315.5 4.4 %copy-start.6 = (s32[4]{0:T(128)}, s32[4]{0:T(128)S(1)}, u32[]{:S(2)}) copy-start(s32[4]{0:T(128)S(1)} %get-tuple-element.1371) | copy-start | bytes 52 | tf_op jit(solution)/shard_map/while
  325.5 2.1 copy-start.7
  327.6 4.4 %copy-start.6 = (s32[4]{0:T(128)}, s32[4]{0:T(128)S(1)}, u32[]{:S(2)}) copy-start(s32[4]{0:T(128)S(1)} %get-tuple-element.1371) | copy-start | bytes 52 | tf_op jit(solution)/shard_map/while
  337.6 2.1 copy-start.7
  339.6 58.8 %collective-permute-start.2 = (f32[33,8192]{1,0:T(8,128)S(1)}, f32[33,8192]{1,0:T(8,128)S(1)}, u32[]{:S(2)}, u32[]{:S(2)}) collective-permute-start(f32[33,8192]{1,0:T(8,128)S(1)} %get-tuple-element.515), channel_id=1, source_target_pairs={{0,4},{4,8},{8,12},{12,16},{16,20},{20,24},{24,28},{1,5},{5,9},{9,... | collective-permute-start | bytes 3244040 | tf_op jit(solution)/shard_map/ppermute | solution.py:17
Sparse Core Ops, SparseCore 0:
  399.8 27.4 reduce-scatter.1
where the time goes:
time: 442 us; the launch traced here: 437 us
  loops' own time  97 us (22%)
  other arithmetic  70.9 us (16%)
  local copies, waits for them, and re-layouts  62.7 us (14%)
  waiting for transfers between devices  58.1 us (13%)
  blocking collectives  55.1 us (12%)
  matrix products  42.9 us (10%)
  starting transfers between devices  32.9 us (7%)
  between operations  16.9 us (4%)
    reduce_sum x30, other arithmetic, item_of(): first_rank = jnp.sum(jnp.where(block_ids == owner_blk, starts_at, 0))  38 us
    another operation x1, loops' own time, body(): row_lse = lax.fori_loop(0, n_items, row_fold, row_empty)  33.4 us
    ppermute x3, waiting for transfers between devices, passed_along(): lax.ppermute(value, axis, [(source, source + steps) for source in range(i...  33.1 us
    ppermute x3, starting transfers between devices, passed_along(): lax.ppermute(value, axis, [(source, source + steps) for source in range(i...  32.9 us
    another operation x1, loops' own time, body(): row_num, col_num = lax.fori_loop(0, n_items, plan_fold, start_sums)  31.7 us
    another operation x1, loops' own time, body(): col_lse = lax.fori_loop(0, n_items, col_fold, col_empty)  31.6 us
    reduce_scatter x1, waiting for transfers between devices, body(): row_num = lax.psum_scatter(row_num, 'blk', scatter_dimension=1, tiled=True)  25 us
    dot_general x30, matrix products, tile_cost(): lax.dot_general(row_block, col_block, (((0,), (0,)), ((), ())), preferred...  22.5 us
  transfers between devices with their start and end apart: 4, of which 3 were waited for; matrix products, arithmetic and copies ran while one was open for 2% of the time, Pallas kernels for 0%

commit v1 on v0

v1 whole, which is shorter than its diff:
```python
import functools
import math

import jax
import jax.numpy as jnp
from jax import lax
from jax.experimental import pallas as pl
from jax.experimental.pallas import tpu as pltpu
from jax.sharding import PartitionSpec as P

TILE = 512
EPSILON = 0.05
LOG2E = math.log2(math.e)
LN2 = math.log(2.0)
NEG = -1e30
UNROLL = 4
HALF = 64
EXT = 48


def split3(value):
    hi = value.astype(jnp.bfloat16).astype(jnp.float32)
    rest = value - hi
    mid = rest.astype(jnp.bfloat16).astype(jnp.float32)
    return hi, mid, rest - mid


def rows_of(pieces, width):
    index = lax.broadcasted_iota(jnp.int32, (8, width), 0)
    block = jnp.zeros((8, width), jnp.float32)
    for place, piece in enumerate(pieces):
        block = jnp.where(index == place, piece, block)
    return block


def sum_squares(cells):
    return jnp.sum(cells * cells, axis=0, keepdims=True)


def own_records(own_ref, xrec, feat, slice_of, tiles_blk, tiles, bias_of):
    width = TILE // (tiles // tiles_blk)
    gain = 2.0 * LOG2E / (feat * EPSILON)
    xrec[...] = jnp.zeros_like(xrec)

    def one(tile, carry):
        start = pl.multiple_of((tile % tiles_blk) * TILE + slice_of * width, width)
        cells = own_ref[tile // tiles_blk, 0:feat, pl.ds(start, width)].astype(jnp.float32)
        scaled = cells * gain
        high = scaled.astype(jnp.bfloat16)
        xrec[tile, 0:feat, :] = high
        xrec[tile, HALF : HALF + feat, :] = (scaled - high.astype(jnp.float32)).astype(jnp.bfloat16)
        bias = split3(bias_of(tile, cells))
        ones = jnp.ones((1, width), jnp.float32)
        aux = rows_of((ones, ones, ones) + bias, width)
        xrec[tile, HALF - 8 : HALF, :] = aux.astype(jnp.bfloat16)
        return carry

    lax.fori_loop(0, tiles, one, 0)


def other_records(other_ref, yrec, build, feat, tiles_blk, tiles, bias_of):
    build[...] = jnp.zeros_like(build)
    ones = jnp.ones((1, TILE), jnp.float32)

    def one(tile, carry):
        start = pl.multiple_of((tile % tiles_blk) * TILE, TILE)
        cells = other_ref[tile // tiles_blk, 0:feat, pl.ds(start, TILE)].astype(jnp.float32)
        build[0:feat, :] = cells
        build[HALF : HALF + feat, :] = cells
        bias = split3(bias_of(tile, start, cells))
        build[HALF - 8 : HALF, :] = rows_of(bias + (ones, ones, ones), TILE)
        yrec[pl.ds(pl.multiple_of(tile * TILE, TILE), TILE), :] = build[...].T.astype(jnp.bfloat16)
        return carry

    lax.fori_loop(0, tiles, one, 0)
    lane = lax.broadcasted_iota(jnp.int32, (TILE, 2 * HALF), 1)
    yrec[tiles * TILE : (tiles + 1) * TILE, :] = jnp.where(lane == HALF - 8, NEG, 0.0).astype(
        jnp.bfloat16
    )


def ext_records(prog_ref, ext, progs, tiles_blk, tiles):
    index = lax.broadcasted_iota(jnp.int32, (EXT - progs, TILE), 0)
    tail = jnp.where(index == 0, 1.0, 0.0).astype(jnp.bfloat16)

    def one(tile, carry):
        start = pl.multiple_of((tile % tiles_blk) * TILE, TILE)
        ext[tile, 0:progs, :] = prog_ref[tile // tiles_blk, :, pl.ds(start, TILE)]
        ext[tile, progs:EXT, :] = tail
        return carry

    lax.fori_loop(0, tiles, one, 0)
    ext[tiles] = jnp.zeros((EXT, TILE), jnp.bfloat16)


def listed_pairs(lists_ref, mine, other, most, blocks, tiles_blk, tiles, own_first):
    def of_block(block, place):
        def one(slot, at):
            row = lists_ref[block, slot] + block * tiles_blk
            col = lists_ref[block, most + slot]
            mine[at] = row if own_first else col
            other[at] = col if own_first else row
            return at + 1

        return lax.fori_loop(0, lists_ref[block, 2 * most], one, place)

    total = lax.fori_loop(0, blocks, of_block, 0)
    last = mine[jnp.maximum(total - 1, 0)]
    for extra in range(UNROLL - 1):
        mine[total + extra] = last
        other[total + extra] = tiles
    return (total + UNROLL - 1) // UNROLL


def scores_of(yrec, xrec, mine, other):
    rows = yrec[pl.ds(pl.multiple_of(other * TILE, TILE), TILE), :]
    return jnp.dot(rows, xrec[mine], preferred_element_type=jnp.float32)


def spread(parts_ref, tile, blocks):
    return jnp.concatenate([parts_ref[block, pl.ds(tile, 1), :] for block in range(blocks)], axis=1)


def row_kernel(dims, lists_ref, own_ref, next_ref, pot_ref, rp_ref, xrec, yrec, build, high, total, mine, other):
    feat, blocks, tiles_blk, most = dims
    tiles = blocks * tiles_blk
    to_score = LOG2E / EPSILON
    groups = listed_pairs(lists_ref, mine, other, most, blocks, tiles_blk, tiles, True)
    own_records(
        own_ref, xrec, feat, lax.axis_index("blk"), tiles_blk, tiles,
        lambda tile, cells: jnp.zeros((1, cells.shape[1]), jnp.float32),
    )

    def bias(tile, start, cells):
        pot = pot_ref[tile // tiles_blk, :, pl.ds(start, TILE)].astype(jnp.float32)
        return (pot - sum_squares(cells) / feat) * to_score

    other_records(next_ref, yrec, build, feat, tiles_blk, tiles, bias)
    high[...] = jnp.full_like(high, NEG)
    total[...] = jnp.zeros_like(total)

    def group(index, carry):
        for step in range(UNROLL):
            at = index * UNROLL + step
            row = mine[at]
            scores = scores_of(yrec, xrec, row, other[at])
            old = high[row]
            new = jnp.maximum(old, jnp.max(scores, axis=0, keepdims=True))
            part = jnp.sum(jnp.exp2(scores - new), axis=0, keepdims=True)
            total[row] = total[row] * jnp.exp2(old - new) + part
            high[row] = new
        return carry

    lax.fori_loop(0, groups, group, 0)
    at_end = lax.axis_index("sec") == lax.axis_size("sec") - 1
    width = TILE // blocks
    for tile in range(tiles):
        start = pl.multiple_of((tile % tiles_blk) * TILE + lax.axis_index("blk") * width, width)
        cells = own_ref[tile // tiles_blk, 0:feat, pl.ds(start, width)].astype(jnp.float32)
        score = high[tile] + jnp.log2(total[tile]) - sum_squares(cells) * (to_score / feat)
        rp_ref[tile : tile + 1, :] = jnp.where(at_end, 0.0, score * (-EPSILON * LN2))


def col_kernel(dims, lists_ref, own_ref, prev_ref, rp_ref, prog_ref, cp_ref, back_ref,
               xrec, yrec, build, ext, high, total, acc, mine, other):
    feat, blocks, tiles_blk, most = dims
    tiles = blocks * tiles_blk
    to_score = LOG2E / EPSILON
    progs = prog_ref.shape[1]
    groups = listed_pairs(lists_ref, mine, other, most, blocks, tiles_blk, tiles, False)
    own_records(
        own_ref, xrec, feat, lax.axis_index("blk"), tiles_blk, tiles,
        lambda tile, cells: jnp.zeros((1, cells.shape[1]), jnp.float32),
    )

    def bias(tile, start, cells):
        return (spread(rp_ref, tile, blocks) - sum_squares(cells) / feat) * to_score

    other_records(prev_ref, yrec, build, feat, tiles_blk, tiles, bias)
    ext_records(prog_ref, ext, progs, tiles_blk, tiles)
    high[...] = jnp.full_like(high, NEG)
    total[...] = jnp.zeros_like(total)
    acc[...] = jnp.zeros_like(acc)

    def group(index, carry):
        for step in range(UNROLL):
            at = index * UNROLL + step
            col, row = mine[at], other[at]
            scores = scores_of(yrec, xrec, col, row)
            old = high[col]
            new = jnp.maximum(old, jnp.max(scores, axis=0, keepdims=True))
            weight = jnp.exp2(scores - new)
            part = jnp.sum(weight, axis=0, keepdims=True)
            shrink = jnp.exp2(old - new)
            sums = jnp.dot(ext[row], weight.astype(jnp.bfloat16), preferred_element_type=jnp.float32)
            acc[col] = acc[col] * shrink + sums
            total[col] = total[col] * shrink + part
            high[col] = new
        return carry

    lax.fori_loop(0, groups, group, 0)
    width = TILE // blocks
    for tile in range(tiles):
        start = pl.multiple_of((tile % tiles_blk) * TILE + lax.axis_index("blk") * width, width)
        cells = own_ref[tile // tiles_blk, 0:feat, pl.ds(start, width)].astype(jnp.float32)
        filled = total[tile] > 0.0
        score = high[tile] + jnp.log2(total[tile]) - sum_squares(cells) * (to_score / feat)
        cp_ref[tile : tile + 1, :] = jnp.where(filled, score * (-EPSILON * LN2), 0.0)
        back_ref[tile] = jnp.where(filled, acc[tile] / total[tile], 0.0)


def plan_kernel(dims, lists_ref, own_ref, next_ref, rp_ref, cp_ref, prog_ref, back_ref, out_ref,
                xrec, yrec, build, ext, acc, mine, other):
    feat, blocks, tiles_blk, most = dims
    tiles = blocks * tiles_blk
    to_score = LOG2E / EPSILON
    progs = prog_ref.shape[1]
    groups = listed_pairs(lists_ref, mine, other, most, blocks, tiles_blk, tiles, True)
    own_records(
        own_ref, xrec, feat, lax.axis_index("blk"), tiles_blk, tiles,
        lambda tile, cells: (rp_ref[pl.ds(tile, 1), :] - sum_squares(cells) / feat) * to_score,
    )

    def bias(tile, start, cells):
        return (spread(cp_ref, tile, blocks) - sum_squares(cells) / feat) * to_score

    other_records(next_ref, yrec, build, feat, tiles_blk, tiles, bias)
    ext_records(prog_ref, ext, progs, tiles_blk, tiles)
    acc[...] = back_ref[...]

    def group(index, carry):
        for step in range(UNROLL):
            at = index * UNROLL + step
            row, col = mine[at], other[at]
            plan = jnp.exp2(scores_of(yrec, xrec, row, col)).astype(jnp.bfloat16)
            acc[row] = acc[row] + jnp.dot(ext[col], plan, preferred_element_type=jnp.float32)
        return carry

    lax.fori_loop(0, groups, group, 0)
    for tile in range(tiles):
        sums = acc[tile]
        out_ref[tile] = (sums[0:progs] / sums[progs : progs + 1]).astype(jnp.bfloat16)


def passed_along(value, steps):
    count = lax.axis_size("sec")
    first, last = max(0, -steps), min(count, count - steps)
    return lax.ppermute(value, "sec", [(source, source + steps) for source in range(first, last)])


def call(kernel, out_shape, operands, scratch):
    specs = [pl.BlockSpec(memory_space=pltpu.SMEM)]
    specs += [pl.BlockSpec(memory_space=pltpu.VMEM)] * (len(operands) - 1)
    outs = jax.tree.map(lambda _: pl.BlockSpec(memory_space=pltpu.VMEM), out_shape)
    return pl.pallas_call(
        kernel, out_shape=out_shape, in_specs=specs, out_specs=outs, scratch_shapes=scratch,
    )(*operands)


def body(features, programs, column_pot, tile_pairs, pair_counts):
    feat, cells_blk = features.shape[1:]
    progs = programs.shape[1]
    tiles_blk = cells_blk // TILE
    most = tile_pairs.shape[2]
    blocks = lax.axis_size("blk")
    tiles = tiles_blk * blocks
    width = TILE // blocks
    dims = (feat, blocks, tiles_blk, most)
    block = lax.axis_index("blk")

    gather = functools.partial(lax.all_gather, axis_name="blk")
    x_next, x_prev = passed_along(features[0], -1), passed_along(features[0], 1)
    lists = gather(jnp.concatenate([tile_pairs[0, 0], tile_pairs[1, 0], pair_counts[0]]))
    own = gather(features[0])
    pot = gather(column_pot)
    nexts = gather(x_next)
    prevs = gather(x_prev)
    prog_next, prog_prev = passed_along(programs[0], -1), passed_along(programs[0], 1)
    prog_next, prog_prev = gather(prog_next), gather(prog_prev)
    lists_prev = passed_along(lists, 1)

    f32, bf16 = jnp.float32, jnp.bfloat16
    xrec = pltpu.VMEM((tiles, 2 * HALF, width), bf16)
    yrec = pltpu.VMEM(((tiles + 1) * TILE, 2 * HALF), bf16)
    build = pltpu.VMEM((2 * HALF, TILE), f32)
    ext = pltpu.VMEM((tiles + 1, EXT, TILE), bf16)
    stat = pltpu.VMEM((tiles, 1, width), f32)
    acc = pltpu.VMEM((tiles, EXT, width), f32)
    index = pltpu.SMEM((blocks * most + UNROLL,), jnp.int32)
    pots = jax.ShapeDtypeStruct((tiles, width), f32)
    sums = jax.ShapeDtypeStruct((tiles, EXT, width), f32)

    row_own = call(
        functools.partial(row_kernel, dims), pots, (lists, own, nexts, pot),
        [xrec, yrec, build, stat, stat, index, index],
    )
    row_all = gather(row_own)
    row_prev = passed_along(row_all, 1)
    col_own, back = call(
        functools.partial(col_kernel, dims), (pots, sums), (lists_prev, own, prevs, row_prev, prog_prev),
        [xrec, yrec, build, ext, stat, stat, acc, index, index],
    )
    col_all = passed_along(gather(col_own), -1)
    smooth = call(
        functools.partial(plan_kernel, dims),
        jax.ShapeDtypeStruct((tiles, progs, width), bf16),
        (lists, own, nexts, row_own, col_all, prog_next, back),
        [xrec, yrec, build, ext, acc, index, index],
    )
    smooth = lax.all_to_all(smooth.reshape(blocks, tiles_blk, progs, width), "blk", 0, 0)
    smoothed = smooth.transpose(2, 1, 0, 3).reshape(1, progs, cells_blk)

    def own_part(parts):
        mine = lax.dynamic_slice_in_dim(parts, block * tiles_blk, tiles_blk, 1)
        return mine.transpose(1, 0, 2).reshape(1, cells_blk)

    return smoothed, own_part(row_all), own_part(col_all)


def solution(mesh):
    in_specs = (
        P("sec", None, "blk"),
        P("sec", None, "blk"),
        P("sec", "blk"),
        P(None, "sec", "blk"),
        P("sec", "blk"),
    )
    out_specs = (P("sec", None, "blk"), P("sec", "blk"), P("sec", "blk"))
    return jax.shard_map(body, mesh=mesh, in_specs=in_specs, out_specs=out_specs, check_vma=False)
```

time: 442 us -> 153 us (0.35); the launches traced: 437 us -> 152 us
  loops' own time: 97 us -> 0 us
  other arithmetic: 70.9 us -> 0.17 us
  local copies, waits for them, and re-layouts: 62.7 us -> 6.68 us
  matrix products: 42.9 us -> 0 us
  waiting for transfers between devices: 58.1 us -> 19.9 us
  Pallas kernels: 0 us -> 31.3 us
  between operations: 16.9 us -> 2.08 us
  blocking collectives: 55.1 us -> 66.7 us
  starting transfers between devices: 32.9 us -> 25.5 us
    another operation x5 -> x0, loops' own time: 97 us -> none  [the longest x1 33.4 us: body(): row_lse = lax.fori_loop(0, n_items, row_fold, row_empty)]
    reduce_sum x82 -> x0, other arithmetic: 61.7 us -> none  [the longest x30 38 us: item_of(): first_rank = jnp.sum(jnp.where(block_ids == owner_blk, starts_at, 0))]
    dynamic_slice x142 -> x0, local copies, waits for them, and re-layouts: 57.6 us -> none  [the longest x20 13.2 us: item_of(): all_pairs[1, 0, slot_index]]
    dot_general x50 -> x0, matrix products: 42.9 us -> none  [the longest x30 22.5 us: tile_cost(): lax.dot_general(row_block, col_block, (((0,), (0,)), ((), ())), preferred...]
    pallas_call x0 -> x3, Pallas kernels: none -> 31.3 us  [call(): pl.pallas_call(kernel, out_shape=out_shape, in_specs=specs, out_specs=out...]
    reduce_scatter x1 -> x0, waiting for transfers between devices: 25 us -> none  [body(): row_num = lax.psum_scatter(row_num, 'blk', scatter_dimension=1, tiled=True)]
    ppermute x3 -> x7, waiting for transfers between devices: 33.1 us -> 16.7 us  [passed_along(): lax.ppermute(value, 'sec', [(source, source + steps) for source in range(...]
    all_gather x8, blocking collectives: 50.6 us -> 61.8 us  [the longest x2 15.4 us: body(): prog_next, prog_prev = (gather(prog_next), gather(prog_prev))]
  transfers between devices with their start and end apart: 4 -> 8, of which waited for: 3 -> 2; matrix products, arithmetic and copies ran while one was open for 2% -> 2% of each run, Pallas kernels for 0% -> 6%
where the time goes in v1:
time: 153 us; the launch traced here: 152 us
  blocking collectives  66.7 us (44%)
  Pallas kernels  31.3 us (20%)
  starting transfers between devices  25.5 us (17%)
  waiting for transfers between devices  19.9 us (13%)
  local copies, waits for them, and re-layouts  6.68 us (4%)
  between operations  2.08 us (1%)
    pallas_call x3, Pallas kernels, call(): pl.pallas_call(kernel, out_shape=out_shape, in_specs=specs, out_specs=out...  31.3 us
    ppermute x7, starting transfers between devices, passed_along(): lax.ppermute(value, 'sec', [(source, source + steps) for source in range(...  22.2 us
    ppermute x7, waiting for transfers between devices, passed_along(): lax.ppermute(value, 'sec', [(source, source + steps) for source in range(...  16.7 us
    all_gather x2, blocking collectives, body(): prog_next, prog_prev = (gather(prog_next), gather(prog_prev))  15.4 us
    all_gather x1, blocking collectives, body(): own = gather(features[0])  10.5 us
    all_gather x1, blocking collectives, body(): nexts = gather(x_next)  9.85 us
    all_gather x1, blocking collectives, body(): prevs = gather(x_prev)  9.58 us
    all_gather x1, blocking collectives, body(): pot = gather(column_pot)  5.62 us
  transfers between devices with their start and end apart: 8, of which 2 were waited for; matrix products, arithmetic and copies ran while one was open for 2% of the time, Pallas kernels for 6%

profile of v1, /device:TPU:0, one launch (start us, length us, event | category | flops | bytes accessed | tf_op | source)
XLA Modules:
  0.0 152.4 jit_solution(16367293260410706091)
XLA Ops:
  0.6 1.3 collective-permute-start
  1.9 5.5 %collective-permute-start.2 = (bf16[52,2048]{1,0:T(8,128)(2,1)}, bf16[52,2048]{1,0:T(8,128)(2,1)S(1)}, u32[]{:S(2)}, u32[]{:S(2)}) collective-permute-start(bf16[52,2048]{1,0:T(8,128)(2,1)} %bitcast.29), channel_id=1, source_target_pairs={{0,4},{4,8},{8,12},{12,16},{16,20},{20,24},{24,28},{1,5},{5,9},{9,... | collective-permute-start | bytes 638984 | tf_op jit(solution)/shard_map/ppermute | solution.py:248
  7.5 4.8 %collective-permute-start.4 = (bf16[32,2048]{1,0:T(8,128)(2,1)}, bf16[32,2048]{1,0:T(8,128)(2,1)S(1)}, u32[]{:S(2)}, u32[]{:S(2)}) collective-permute-start(bf16[32,2048]{1,0:T(8,128)(2,1)} %bitcast.38), channel_id=1, source_target_pairs={{0,4},{4,8},{8,12},{12,16},{16,20},{20,24},{24,28},{1,5},{5,9},{9,... | collective-permute-start | bytes 393224 | tf_op jit(solution)/shard_map/ppermute | solution.py:248
  12.3 1.3 collective-permute-start.6
  13.6 0.0 copy-start.5
  13.6 0.7 copy-done.5
  14.9 0.0 copy-start.6
  14.9 0.6 copy-done.6
  15.6 0.6 dynamic-slice
  16.8 0.2 add_dynamic-update-slice_fusion
  17.0 4.9 %all-reduce = s32[228]{0:T(256)S(1)} all-reduce(s32[228]{0:T(256)S(1)} %add_dynamic-update-slice_fusion), channel_id=2, replica_groups=mesh['sec'=8,'blk'=4] {'blk'}, use_global_device_ids=true, to_apply=%add | all-reduce | flops 228 | bytes 1824
  21.9 0.1 reshape.22.lists_ref
  22.0 0.0 copy-start.2
  22.0 4.5 %collective-permute-start.1 = (s32[4,57]{1,0:T(4,128)S(1)}, s32[4,57]{1,0:T(4,128)S(1)}, u32[]{:S(2)}, u32[]{:S(2)}) collective-permute-start(s32[4,57]{1,0:T(4,128)S(1)} %reshape.22.lists_ref), channel_id=1, source_target_pairs={{0,4},{4,8},{8,12},{12,16},{16,20},{20,24},{24,28},{1,5},{5,9},{9,... | collective-permute-start | bytes 2744 | tf_op jit(solution)/shard_map/ppermute | solution.py:248
  26.6 10.5 %all_gather.53.own_ref = bf16[4,52,2048]{2,1,0:T(8,128)(2,1)} all-gather(bf16[1,52,2048]{2,1,0:T(8,128)(2,1)} %param.5), channel_id=1, replica_groups=mesh['sec'=8,'blk'=4] {'blk'}, dimensions={0}, use_global_device_ids=true | all-gather | bytes 1064960 | tf_op jit(solution)/shard_map/all_gather | solution.py:274
  37.1 0.0 copy-done.2
  37.1 0.0 copy-start.3
  37.1 0.7 copy-done.3
  37.8 5.6 %all-gather.9.pot_ref = bf16[4,1,2048]{2,1,0:T(2,128)(2,1)} all-gather(bf16[1,1,2048]{2,1,0:T(2,128)(2,1)S(1)} %bitcast.35), channel_id=4, replica_groups=mesh['sec'=8,'blk'=4] {'blk'}, dimensions={0}, use_global_device_ids=true | all-gather | bytes 20480 | tf_op jit(solution)/shard_map/all_gather | solution.py:275
  43.4 0.0 collective-permute-done.4
  43.4 7.7 %all-gather.5 = bf16[128,2048]{1,0:T(8,128)(2,1)} all-gather(bf16[32,2048]{1,0:T(8,128)(2,1)S(1)} %collective-permute-done.4), channel_id=7, replica_groups=mesh['sec'=8,'blk'=4] {'blk'}, dimensions={0}, use_global_device_ids=true | all-gather | bytes 655360 | tf_op jit(solution)/shard_map/all_gather | solution.py:279
  51.1 0.0 collective-permute-done.6
  51.1 7.7 %all-gather.7 = bf16[128,2048]{1,0:T(8,128)(2,1)} all-gather(bf16[32,2048]{1,0:T(8,128)(2,1)S(1)} %collective-permute-done.6), channel_id=9, replica_groups=mesh['sec'=8,'blk'=4] {'blk'}, dimensions={0}, use_global_device_ids=true | all-gather | bytes 655360 | tf_op jit(solution)/shard_map/all_gather | solution.py:279
  58.8 0.0 collective-permute-done
  58.8 9.9 %all-gather.8.next_ref = bf16[4,52,2048]{2,1,0:T(8,128)(2,1)} all-gather(bf16[1,52,2048]{2,1,0:T(8,128)(2,1)S(1)} %bitcast.31), channel_id=3, replica_groups=mesh['sec'=8,'blk'=4] {'blk'}, dimensions={0}, use_global_device_ids=true | all-gather | bytes 1064960 | tf_op jit(solution)/shard_map/all_gather | solution.py:276
  68.7 9.9 %shard_map.76.rp_ref = f32[16,128]{1,0:T(8,128)} custom-call(s32[4,57]{1,0:T(4,128)} %copy-done.2, bf16[4,52,2048]{2,1,0:T(8,128)(2,1)} %all_gather.53.own_ref, bf16[4,52,2048]{2,1,0:T(8,128)(2,1)} %all-gather.8.next_ref, bf16[4,1,2048]{2,1,0:T(2,128)(2,1)} %all-gather.9.pot_ref), custom_call_target="tpu_custom_call" | custom-call | tf_op jit(solution)/shard_map/pallas_call | solution.py:255
  78.6 5.4 %all-gather.4 = f32[64,128]{1,0:T(8,128)S(1)} all-gather(f32[16,128]{1,0:T(8,128)} %shard_map.76.rp_ref), channel_id=6, replica_groups=mesh['sec'=8,'blk'=4] {'blk'}, dimensions={0}, use_global_device_ids=true | all-gather | bytes 40960 | tf_op jit(solution)/shard_map/all_gather | solution.py:297
  84.0 3.5 %collective-permute-start.3 = (f32[4,16,128]{2,1,0:T(8,128)S(1)}, f32[4,16,128]{2,1,0:T(8,128)S(1)}, u32[]{:S(2)}, u32[]{:S(2)}) collective-permute-start(f32[4,16,128]{2,1,0:T(8,128)S(1)} %bitcast.32), channel_id=1, source_target_pairs={{0,4},{4,8},{8,12},{12,16},{16,20},{20,24},{24,28},{1,5},{5,9},{9,... | collective-permute-start | bytes 98312 | tf_op jit(solution)/shard_map/ppermute | solution.py:248
  87.4 0.0 collective-permute-done.2
  87.4 9.6 %all-gather.10.prev_ref = bf16[4,52,2048]{2,1,0:T(8,128)(2,1)} all-gather(bf16[1,52,2048]{2,1,0:T(8,128)(2,1)S(1)} %bitcast.30), channel_id=5, replica_groups=mesh['sec'=8,'blk'=4] {'blk'}, dimensions={0}, use_global_device_ids=true | all-gather | bytes 1064960 | tf_op jit(solution)/shard_map/all_gather | solution.py:277
  97.0 0.0 collective-permute-done.1.lists_ref
  97.0 0.0 copy-start.4
  97.0 0.0 collective-permute-done.3.rp_ref
  97.0 0.0 copy-start.1
  97.0 0.6 copy-done.4
  97.6 0.0 copy-done.1
  97.6 5.2 %shard_map.77 = (f32[16,128]{1,0:T(8,128)}, f32[16,48,128]{2,1,0:T(8,128)}) custom-call(s32[4,57]{1,0:T(4,128)} %copy-done.4, bf16[4,52,2048]{2,1,0:T(8,128)(2,1)} %all_gather.53.own_ref, bf16[4,52,2048]{2,1,0:T(8,128)(2,1)} %all-gather.10.prev_ref, f32[4,16,128]{2,1,0:T(8,128)} %copy-done.1, bf16[4,32,2048]{2,1,0:T(8,128)(2,1)} %bitcast.25), custom_call_target="tpu_custom_call" | custom-call | tf_op jit(solution)/shard_map/pallas_call | solution.py:255
  102.8 5.4 %all-gather.6 = f32[64,128]{1,0:T(8,128)S(1)} all-gather(f32[16,128]{1,0:T(8,128)} %get-tuple-element.5), channel_id=8, replica_groups=mesh['sec'=8,'blk'=4] {'blk'}, dimensions={0}, use_global_device_ids=true | all-gather | bytes 40960 | tf_op jit(solution)/shard_map/all_gather | solution.py:303
  108.2 1.3 collective-permute-start.5
  109.5 0.6 copy.13
  110.1 16.7 %collective-permute-done.5.cp_ref = f32[4,16,128]{2,1,0:T(8,128)S(1)} collective-permute-done((f32[4,16,128]{2,1,0:T(8,128)S(1)}, f32[4,16,128]{2,1,0:T(8,128)S(1)}, u32[]{:S(2)}, u32[]{:S(2)}) %collective-permute-start.5) | collective-permute-done | bytes 32800 | tf_op jit(solution)/shard_map/ppermute | solution.py:248
  126.8 0.0 copy-start
  126.8 0.6 copy-done
  127.4 16.2 %shard_map.78 = bf16[16,32,128]{2,1,0:T(8,128)(2,1)} custom-call(s32[4,57]{1,0:T(4,128)} %copy-done.2, bf16[4,52,2048]{2,1,0:T(8,128)(2,1)} %all_gather.53.own_ref, bf16[4,52,2048]{2,1,0:T(8,128)(2,1)} %all-gather.8.next_ref, f32[16,128]{1,0:T(8,128)} %shard_map.76.rp_ref, f32[4,16,128]{2,1,0:T(8,128)} %copy-done, bf16[4,32,2048]{2,1,0:T(8,128)(2,1)} %bitcast.24, ...), custom_call_target="tpu_custom_call" | custom-call | tf_op jit(solution)/shard_map/pallas_call | solution.py:255
  143.6 3.3 %all-to-all-start = ((bf16[4,4,32,128]{3,2,1,0:T(8,128)(2,1)}), bf16[4,4,32,128]{3,2,1,0:T(8,128)(2,1)S(1)}, u32[]{:S(2)}, u32[]{:S(2)}) async-start(bf16[4,4,32,128]{3,2,1,0:T(8,128)(2,1)} %bitcast.26), calls=%async_computation | async-start | bytes 262144 | tf_op jit(solution)/shard_map/all_to_all | solution.py:310
  147.0 0.7 dynamic-slice_bitcast_fusion
  147.7 0.6 copy.14
  148.3 3.2 %all-to-all-done = bf16[4,4,32,128]{3,2,1,0:T(8,128)(2,1)S(1)} async-done(((bf16[4,4,32,128]{3,2,1,0:T(8,128)(2,1)}), bf16[4,4,32,128]{3,2,1,0:T(8,128)(2,1)S(1)}, u32[]{:S(2)}, u32[]{:S(2)}) %all-to-all-start) | async-done | bytes 131104 | tf_op jit(solution)/shard_map/all_to_all | solution.py:310
  151.5 0.1 copy.12
  151.6 0.7 reshape.19
  (3 shorter events, 0.0 us)
Async XLA Ops:
  0.6 58.2 %collective-permute-start = (bf16[52,2048]{1,0:T(8,128)(2,1)}, bf16[52,2048]{1,0:T(8,128)(2,1)S(1)}, u32[]{:S(2)}, u32[]{:S(2)}) collective-permute-start(bf16[52,2048]{1,0:T(8,128)(2,1)} %bitcast.28), channel_id=1, source_target_pairs={{4,0},{8,4},{12,8},{16,12},{20,16},{24,20},{28,24},{5,1},{9,5},{13... | collective-permute-start | bytes 638984 | tf_op jit(solution)/shard_map/ppermute | solution.py:248
  1.9 85.5 %collective-permute-start.2 = (bf16[52,2048]{1,0:T(8,128)(2,1)}, bf16[52,2048]{1,0:T(8,128)(2,1)S(1)}, u32[]{:S(2)}, u32[]{:S(2)}) collective-permute-start(bf16[52,2048]{1,0:T(8,128)(2,1)} %bitcast.29), channel_id=1, source_target_pairs={{0,4},{4,8},{8,12},{12,16},{16,20},{20,24},{24,28},{1,5},{5,9},{9,... | collective-permute-start | bytes 638984 | tf_op jit(solution)/shard_map/ppermute | solution.py:248
  7.5 35.9 %collective-permute-start.4 = (bf16[32,2048]{1,0:T(8,128)(2,1)}, bf16[32,2048]{1,0:T(8,128)(2,1)S(1)}, u32[]{:S(2)}, u32[]{:S(2)}) collective-permute-start(bf16[32,2048]{1,0:T(8,128)(2,1)} %bitcast.38), channel_id=1, source_target_pairs={{0,4},{4,8},{8,12},{12,16},{16,20},{20,24},{24,28},{1,5},{5,9},{9,... | collective-permute-start | bytes 393224 | tf_op jit(solution)/shard_map/ppermute | solution.py:248
  12.3 38.8 %collective-permute-start.6 = (bf16[32,2048]{1,0:T(8,128)(2,1)}, bf16[32,2048]{1,0:T(8,128)(2,1)S(1)}, u32[]{:S(2)}, u32[]{:S(2)}) collective-permute-start(bf16[32,2048]{1,0:T(8,128)(2,1)} %bitcast.39), channel_id=1, source_target_pairs={{4,0},{8,4},{12,8},{16,12},{20,16},{24,20},{28,24},{5,1},{9,5},{13... | collective-permute-start | bytes 393224 | tf_op jit(solution)/shard_map/ppermute | solution.py:248
  13.6 0.7 copy-start.5
  14.9 0.7 copy-start.6
  22.0 15.1 %copy-start.2 = (s32[4,57]{1,0:T(4,128)}, s32[4,57]{1,0:T(4,128)S(1)}, u32[]{:S(2)}) copy-start(s32[4,57]{1,0:T(4,128)S(1)} %reshape.22.lists_ref) | copy-start | bytes 2740
  22.0 75.0 %collective-permute-start.1 = (s32[4,57]{1,0:T(4,128)S(1)}, s32[4,57]{1,0:T(4,128)S(1)}, u32[]{:S(2)}, u32[]{:S(2)}) collective-permute-start(s32[4,57]{1,0:T(4,128)S(1)} %reshape.22.lists_ref), channel_id=1, source_target_pairs={{0,4},{4,8},{8,12},{12,16},{16,20},{20,24},{24,28},{1,5},{5,9},{9,... | collective-permute-start | bytes 2744 | tf_op jit(solution)/shard_map/ppermute | solution.py:248
  37.1 0.7 copy-start.3
  84.0 13.1 %collective-permute-start.3 = (f32[4,16,128]{2,1,0:T(8,128)S(1)}, f32[4,16,128]{2,1,0:T(8,128)S(1)}, u32[]{:S(2)}, u32[]{:S(2)}) collective-permute-start(f32[4,16,128]{2,1,0:T(8,128)S(1)} %bitcast.32), channel_id=1, source_target_pairs={{0,4},{4,8},{8,12},{12,16},{16,20},{20,24},{24,28},{1,5},{5,9},{9,... | collective-permute-start | bytes 98312 | tf_op jit(solution)/shard_map/ppermute | solution.py:248
  97.0 0.6 copy-start.4
  97.0 0.6 copy-start.1
  108.2 18.6 %collective-permute-start.5 = (f32[4,16,128]{2,1,0:T(8,128)S(1)}, f32[4,16,128]{2,1,0:T(8,128)S(1)}, u32[]{:S(2)}, u32[]{:S(2)}) collective-permute-start(f32[4,16,128]{2,1,0:T(8,128)S(1)} %bitcast.34), channel_id=1, source_target_pairs={{4,0},{8,4},{12,8},{16,12},{20,16},{24,20},{28,24},{5,1},{9,5},{13... | collective-permute-start | bytes 98312 | tf_op jit(solution)/shard_map/ppermute | solution.py:248
  126.8 0.6 copy-start
  143.6 7.9 %all-to-all-start = ((bf16[4,4,32,128]{3,2,1,0:T(8,128)(2,1)}), bf16[4,4,32,128]{3,2,1,0:T(8,128)(2,1)S(1)}, u32[]{:S(2)}, u32[]{:S(2)}) async-start(bf16[4,4,32,128]{3,2,1,0:T(8,128)(2,1)} %bitcast.26), calls=%async_computation | async-start | bytes 262144 | tf_op jit(solution)/shard_map/all_to_all | solution.py:310

commit v2 on v1

v2 whole, which is shorter than its diff:
```python
import functools
import math

import jax
import jax.numpy as jnp
from jax import lax
from jax.experimental import pallas as pl
from jax.experimental.pallas import tpu as pltpu
from jax.sharding import PartitionSpec as P

TILE = 512
EPSILON = 0.05
LOG2E = math.log2(math.e)
LN2 = math.log(2.0)
NEG = -1e30
UNROLL = 4
HALF = 64
EXT = 48


def split3(value):
    hi = value.astype(jnp.bfloat16).astype(jnp.float32)
    rest = value - hi
    mid = rest.astype(jnp.bfloat16).astype(jnp.float32)
    return hi, mid, rest - mid


def rows_of(pieces, width):
    index = lax.broadcasted_iota(jnp.int32, (8, width), 0)
    block = jnp.zeros((8, width), jnp.float32)
    for place, piece in enumerate(pieces):
        block = jnp.where(index == place, piece, block)
    return block


def sum_squares(cells):
    return jnp.sum(cells * cells, axis=0, keepdims=True)


def own_records(own_ref, xrec, feat, tiles_blk, tiles, bias_of):
    width = TILE // (tiles // tiles_blk)
    gain = 2.0 * LOG2E / (feat * EPSILON)
    xrec[...] = jnp.zeros_like(xrec)

    def one(tile, carry):
        cells = own_ref[tile // tiles_blk, tile % tiles_blk].astype(jnp.float32)
        scaled = cells * gain
        high = scaled.astype(jnp.bfloat16)
        xrec[tile, 0:feat, :] = high
        xrec[tile, HALF : HALF + feat, :] = (scaled - high.astype(jnp.float32)).astype(jnp.bfloat16)
        bias = split3(bias_of(tile, cells))
        ones = jnp.ones((1, width), jnp.float32)
        aux = rows_of((ones, ones, ones) + bias, width)
        xrec[tile, HALF - 8 : HALF, :] = aux.astype(jnp.bfloat16)
        return carry

    lax.fori_loop(0, tiles, one, 0)


def other_records(other_ref, yrec, build, feat, tiles_blk, tiles, bias_of):
    build[...] = jnp.zeros_like(build)
    ones = jnp.ones((1, TILE), jnp.float32)

    def one(tile, carry):
        start = pl.multiple_of((tile % tiles_blk) * TILE, TILE)
        cells = other_ref[tile // tiles_blk, 0:feat, pl.ds(start, TILE)].astype(jnp.float32)
        build[0:feat, :] = cells
        build[HALF : HALF + feat, :] = cells
        bias = split3(bias_of(tile, start, cells))
        build[HALF - 8 : HALF, :] = rows_of(bias + (ones, ones, ones), TILE)
        yrec[pl.ds(pl.multiple_of(tile * TILE, TILE), TILE), :] = build[...].T.astype(jnp.bfloat16)
        return carry

    lax.fori_loop(0, tiles, one, 0)
    lane = lax.broadcasted_iota(jnp.int32, (TILE, 2 * HALF), 1)
    yrec[tiles * TILE : (tiles + 1) * TILE, :] = jnp.where(lane == HALF - 8, NEG, 0.0).astype(
        jnp.bfloat16
    )


def ext_records(prog_ref, ext, progs, tiles_blk, tiles):
    index = lax.broadcasted_iota(jnp.int32, (EXT - progs, TILE), 0)
    tail = jnp.where(index == 0, 1.0, 0.0).astype(jnp.bfloat16)

    def one(tile, carry):
        start = pl.multiple_of((tile % tiles_blk) * TILE, TILE)
        ext[tile, 0:progs, :] = prog_ref[tile // tiles_blk, :, pl.ds(start, TILE)]
        ext[tile, progs:EXT, :] = tail
        return carry

    lax.fori_loop(0, tiles, one, 0)
    ext[tiles] = jnp.zeros((EXT, TILE), jnp.bfloat16)


def listed_pairs(lists_ref, mine, other, most, blocks, tiles_blk, tiles, own_first, used=True):
    def of_block(block, place):
        def one(slot, at):
            row = lists_ref[block, 0, slot] + block * tiles_blk
            col = lists_ref[block, 0, most + slot]
            mine[at] = row if own_first else col
            other[at] = col if own_first else row
            return at + 1

        return lax.fori_loop(0, jnp.where(used, lists_ref[block, 0, 2 * most], 0), one, place)

    total = lax.fori_loop(0, blocks, of_block, 0)
    last = mine[jnp.maximum(total - 1, 0)]
    for extra in range(UNROLL - 1):
        mine[total + extra] = last
        other[total + extra] = tiles
    return (total + UNROLL - 1) // UNROLL


def scores_of(yrec, xrec, mine, other):
    rows = yrec[pl.ds(pl.multiple_of(other * TILE, TILE), TILE), :]
    return jnp.dot(rows, xrec[mine], preferred_element_type=jnp.float32)


def spread(parts_ref, tile, blocks, tiles_blk):
    parts = [parts_ref[block, tile // tiles_blk, pl.ds(tile % tiles_blk, 1), :] for block in range(blocks)]
    return jnp.concatenate(parts, axis=1)


def near_side(forward):
    odd = lax.axis_index("sec") % 2
    return odd if forward else 1 - odd


def row_kernel(dims, lists_ref, own_ref, next_ref, pot_ref, rp_ref, xrec, yrec, build, high, total, mine, other):
    feat, blocks, tiles_blk, most = dims
    tiles = blocks * tiles_blk
    to_score = LOG2E / EPSILON
    groups = listed_pairs(lists_ref, mine, other, most, blocks, tiles_blk, tiles, True)
    own_records(
        own_ref, xrec, feat, tiles_blk, tiles,
        lambda tile, cells: jnp.zeros((1, cells.shape[1]), jnp.float32),
    )

    def bias(tile, start, cells):
        pot = pot_ref[tile // tiles_blk, :, pl.ds(start, TILE)].astype(jnp.float32)
        return (pot - sum_squares(cells) / feat) * to_score

    other_records(next_ref.at[near_side(True)], yrec, build, feat, tiles_blk, tiles, bias)
    high[...] = jnp.full_like(high, NEG)
    total[...] = jnp.zeros_like(total)

    def group(index, carry):
        for step in range(UNROLL):
            at = index * UNROLL + step
            row = mine[at]
            scores = scores_of(yrec, xrec, row, other[at])
            old = high[row]
            new = jnp.maximum(old, jnp.max(scores, axis=0, keepdims=True))
            part = jnp.sum(jnp.exp2(scores - new), axis=0, keepdims=True)
            total[row] = total[row] * jnp.exp2(old - new) + part
            high[row] = new
        return carry

    lax.fori_loop(0, groups, group, 0)
    at_end = lax.axis_index("sec") == lax.axis_size("sec") - 1
    for tile in range(tiles):
        cells = own_ref[tile // tiles_blk, tile % tiles_blk].astype(jnp.float32)
        score = high[tile] + jnp.log2(total[tile]) - sum_squares(cells) * (to_score / feat)
        rp_ref[tile // tiles_blk, tile % tiles_blk : tile % tiles_blk + 1, :] = jnp.where(at_end, 0.0, score * (-EPSILON * LN2))


def col_kernel(dims, lists_ref, own_ref, prev_ref, rp_ref, prog_ref, cp_ref, back_ref,
               xrec, yrec, build, ext, high, total, acc, mine, other):
    feat, blocks, tiles_blk, most = dims
    tiles = blocks * tiles_blk
    to_score = LOG2E / EPSILON
    progs = prog_ref.shape[2]
    used = lax.axis_index("sec") > 0
    groups = listed_pairs(
        lists_ref.at[near_side(False)], mine, other, most, blocks, tiles_blk, tiles, False, used
    )
    own_records(
        own_ref, xrec, feat, tiles_blk, tiles,
        lambda tile, cells: jnp.zeros((1, cells.shape[1]), jnp.float32),
    )

    def bias(tile, start, cells):
        return (spread(rp_ref, tile, blocks, tiles_blk) - sum_squares(cells) / feat) * to_score

    other_records(prev_ref.at[near_side(False)], yrec, build, feat, tiles_blk, tiles, bias)
    ext_records(prog_ref.at[near_side(False)], ext, progs, tiles_blk, tiles)
    high[...] = jnp.full_like(high, NEG)
    total[...] = jnp.zeros_like(total)
    acc[...] = jnp.zeros_like(acc)

    def group(index, carry):
        for step in range(UNROLL):
            at = index * UNROLL + step
            col, row = mine[at], other[at]
            scores = scores_of(yrec, xrec, col, row)
            old = high[col]
            new = jnp.maximum(old, jnp.max(scores, axis=0, keepdims=True))
            weight = jnp.exp2(scores - new)
            part = jnp.sum(weight, axis=0, keepdims=True)
            shrink = jnp.exp2(old - new)
            sums = jnp.dot(ext[row], weight.astype(jnp.bfloat16), preferred_element_type=jnp.float32)
            acc[col] = acc[col] * shrink + sums
            total[col] = total[col] * shrink + part
            high[col] = new
        return carry

    lax.fori_loop(0, groups, group, 0)
    for tile in range(tiles):
        cells = own_ref[tile // tiles_blk, tile % tiles_blk].astype(jnp.float32)
        filled = total[tile] > 0.0
        score = high[tile] + jnp.log2(total[tile]) - sum_squares(cells) * (to_score / feat)
        cp_ref[tile // tiles_blk, tile % tiles_blk : tile % tiles_blk + 1, :] = jnp.where(filled, score * (-EPSILON * LN2), 0.0)
        back_ref[tile] = jnp.where(filled, acc[tile] / total[tile], 0.0)


def plan_kernel(dims, lists_ref, own_ref, next_ref, rp_ref, cp_ref, prog_ref, back_ref, out_ref,
                xrec, yrec, build, ext, acc, mine, other):
    feat, blocks, tiles_blk, most = dims
    tiles = blocks * tiles_blk
    to_score = LOG2E / EPSILON
    progs = prog_ref.shape[2]
    groups = listed_pairs(lists_ref, mine, other, most, blocks, tiles_blk, tiles, True)
    own_records(
        own_ref, xrec, feat, tiles_blk, tiles,
        lambda tile, cells: (rp_ref[tile // tiles_blk, pl.ds(tile % tiles_blk, 1), :] - sum_squares(cells) / feat) * to_score,
    )

    def bias(tile, start, cells):
        return (spread(cp_ref, tile, blocks, tiles_blk) - sum_squares(cells) / feat) * to_score

    other_records(next_ref.at[near_side(True)], yrec, build, feat, tiles_blk, tiles, bias)
    ext_records(prog_ref.at[near_side(True)], ext, progs, tiles_blk, tiles)
    acc[...] = back_ref[...]

    def group(index, carry):
        for step in range(UNROLL):
            at = index * UNROLL + step
            row, col = mine[at], other[at]
            plan = jnp.exp2(scores_of(yrec, xrec, row, col)).astype(jnp.bfloat16)
            acc[row] = acc[row] + jnp.dot(ext[col], plan, preferred_element_type=jnp.float32)
        return carry

    lax.fori_loop(0, groups, group, 0)
    for tile in range(tiles):
        sums = acc[tile]
        out_ref[tile // tiles_blk, tile % tiles_blk] = (sums[0:progs] / sums[progs : progs + 1]).astype(jnp.bfloat16)


MESH = pl.DeviceIdType.MESH


def greet(targets):
    barrier = pltpu.get_barrier_semaphore()
    expected = jnp.int32(0)
    for used, sec, blk in targets:

        @pl.when(used)
        def _():
            pl.semaphore_signal(barrier, inc=1, device_id=(sec, blk), device_id_type=MESH)

        expected = expected + jnp.where(used, 1, 0)
    pl.semaphore_wait(barrier, expected)


def send(src, dst, sems, place, sec, blk):
    return pltpu.make_async_remote_copy(
        src_ref=src, dst_ref=dst, send_sem=sems[0].at[place], recv_sem=sems[1].at[place],
        device_id=(sec, blk), device_id_type=MESH,
    )


STAGES = 8


def gather_kernel(counts, x_ref, prog_ref, pot_ref, list_ref, own_ref, xs_ref, progs_ref, pots_ref, lists_ref,
                  all_lists_ref, send_sem, recv_sem, mate_send, mate_recv):
    n_sec, blocks = counts
    sec, blk = lax.axis_index("sec"), lax.axis_index("blk")
    even = sec % 2 == 0
    partner = jnp.where(even, sec + 1, sec - 1)
    relay_to = jnp.where(even, sec + 2, sec - 2)
    relay_from = jnp.where(even, sec - 2, sec + 2)
    has_to = jnp.logical_and(relay_to >= 0, relay_to < n_sec)
    has_from = jnp.logical_and(relay_from >= 0, relay_from < n_sec)
    core = blk + 1 - 2 * (blk % 2)
    across = (blk + 2) % blocks
    corner = core + 2 - 4 * (core // 2)
    mates = (core, across, corner)
    yes = sec >= 0
    greet(
        [(yes, partner, blk), (has_to, relay_to, blk), (has_from, relay_from, blk)]
        + [(yes, sec, mate) for mate in mates]
    )
    sems, mate_sems = (send_sem, recv_sem), (mate_send, mate_recv)
    width = TILE // blocks
    tiles_blk = x_ref.shape[1] // TILE
    half = x_ref.shape[1] // 2
    sources = [
        (list_ref, lists_ref, None), (x_ref, xs_ref, 0), (x_ref, xs_ref, 1), (prog_ref, progs_ref, 0), (prog_ref, progs_ref, 1),
    ]

    def cut(ref, part):
        return ref if part is None else ref.at[:, part * half : (part + 1) * half]

    def place_of(buffer, side, owner, part):
        return cut(buffer.at[side, owner], part)

    def first(c):
        src, buffer, part = sources[c]
        return send(cut(src, part), place_of(buffer, 0, blk, part), sems, STAGES * c, partner, blk)

    def relay(c):
        _, buffer, part = sources[c]
        return send(
            place_of(buffer, 0, blk, part), place_of(buffer, 1, blk, part), sems, STAGES * c + 1, relay_to, blk
        )

    def share(c, side, kind):
        _, buffer, part = sources[c]
        owner = across if kind == 2 else blk
        slot = place_of(buffer, side, owner, part)
        return send(slot, slot, sems, STAGES * c + 2 + 3 * side + kind, sec, across if kind == 0 else core)

    def to_mate(k):
        mate = mates[k]
        copies = []
        for tile in range(tiles_blk):
            start = pl.multiple_of(tile * TILE + mate * width, width)
            copies.append((x_ref.at[:, pl.ds(start, width)], own_ref.at[blk, tile]))
        copies.append((pot_ref, pots_ref.at[blk]))
        copies.append((list_ref, all_lists_ref.at[blk]))
        per = len(copies)
        return [send(src, dst, mate_sems, per * k + n, sec, mate) for n, (src, dst) in enumerate(copies)]

    chunks = range(len(sources))
    for c in chunks:
        first(c).start()
    for k in range(3):
        for copy in to_mate(k):
            copy.start()
    for tile in range(tiles_blk):
        start = pl.multiple_of(tile * TILE + blk * width, width)
        own_ref[blk, tile] = x_ref[:, pl.ds(start, width)]
    pots_ref[blk] = pot_ref[...]
    all_lists_ref[blk] = list_ref[...]
    for c in chunks:
        first(c).wait_recv()

        @pl.when(has_to)
        def _():
            relay(c).start()

        share(c, 0, 0).start()
        share(c, 0, 1).start()
    for c in chunks:
        share(c, 0, 0).wait_recv()
        share(c, 0, 2).start()

        @pl.when(has_from)
        def _():
            relay(c).wait_recv()
            share(c, 1, 0).start()
            share(c, 1, 1).start()

    @pl.when(has_from)
    def _():
        for c in chunks:
            share(c, 1, 0).wait_recv()
            share(c, 1, 2).start()

    for c in chunks:
        for kind in (1, 2):
            share(c, 0, kind).wait_recv()

    @pl.when(has_from)
    def _():
        for c in chunks:
            for kind in (1, 2):
                share(c, 1, kind).wait_recv()

    for k in range(3):
        for copy in to_mate(k):
            copy.wait_recv()
    for c in chunks:
        first(c).wait_send()
        for kind in range(3):
            share(c, 0, kind).wait_send()

    @pl.when(has_to)
    def _():
        for c in chunks:
            relay(c).wait_send()

    @pl.when(has_from)
    def _():
        for c in chunks:
            for kind in range(3):
                share(c, 1, kind).wait_send()

    for k in range(3):
        for copy in to_mate(k):
            copy.wait_send()


def shift_kernel(counts, steps, part_ref, out_ref, send_sem, recv_sem):
    n_sec, blocks = counts
    sec, blk = lax.axis_index("sec"), lax.axis_index("blk")
    to, source = sec + steps, sec - steps
    has_to = jnp.logical_and(to >= 0, to < n_sec)
    has_from = jnp.logical_and(source >= 0, source < n_sec)
    targets = [(blk + turn) % blocks for turn in range(blocks)]
    greet([(has_to, to, mate) for mate in targets] + [(has_from, source, mate) for mate in targets])

    def copy(turn):
        return send(part_ref, out_ref.at[blk], (send_sem, recv_sem), turn, to, targets[turn])

    def arrival(turn):
        slot = out_ref.at[(blk + blocks - turn) % blocks]
        return send(part_ref, slot, (send_sem, recv_sem), turn, to, targets[turn])

    @pl.when(has_to)
    def _():
        for turn in range(blocks):
            copy(turn).start()

    @pl.when(has_from)
    def _():
        for turn in range(blocks):
            arrival(turn).wait_recv()

    @pl.when(jnp.logical_not(has_from))
    def _():
        out_ref[...] = jnp.zeros_like(out_ref)

    @pl.when(has_to)
    def _():
        for turn in range(blocks):
            copy(turn).wait_send()


def return_kernel(counts, smooth_ref, row_ref, col_ref, out_ref, rows_ref, cols_ref, parts, send_sem, recv_sem):
    n_sec, blocks = counts
    sec, blk = lax.axis_index("sec"), lax.axis_index("blk")
    tiles_blk, width = row_ref.shape[1:]
    mates = [(blk + turn) % blocks for turn in range(blocks)]
    greet([(sec >= 0, sec, mate) for mate in mates[1:]])
    sems = (send_sem, recv_sem)
    per = tiles_blk + 1

    def copies(turn, arriving):
        mate = mates[turn]
        owner = (blk + blocks - turn) % blocks if arriving else blk
        pairs = []
        for tile in range(tiles_blk):
            start = pl.multiple_of(tile * TILE + owner * width, width)
            pairs.append((smooth_ref.at[mate, tile], out_ref.at[:, pl.ds(start, width)]))
        pairs.append((row_ref.at[mate], parts.at[owner]))
        return [send(src, dst, sems, per * (turn - 1) + n, sec, mate) for n, (src, dst) in enumerate(pairs)]

    for turn in range(1, blocks):
        for copy in copies(turn, False):
            copy.start()
    for tile in range(tiles_blk):
        start = pl.multiple_of(tile * TILE + blk * width, width)
        out_ref[:, pl.ds(start, width)] = smooth_ref[blk, tile]
    parts[blk] = row_ref[blk]
    for owner in range(blocks):
        for tile in range(tiles_blk):
            start = tile * TILE + owner * width
            cols_ref[:, start : start + width] = col_ref[owner, blk, tile : tile + 1, :]
    for turn in range(1, blocks):
        for copy in copies(turn, True):
            copy.wait_recv()
    for owner in range(blocks):
        for tile in range(tiles_blk):
            start = tile * TILE + owner * width
            rows_ref[:, start : start + width] = parts[owner, tile : tile + 1, :]
    for turn in range(1, blocks):
        for copy in copies(turn, False):
            copy.wait_send()


def in_vmem(count):
    return [pl.BlockSpec(memory_space=pltpu.VMEM)] * count


def exchange(kernel, number, out_shape, operands, scratch):
    outs = jax.tree.map(lambda _: pl.BlockSpec(memory_space=pltpu.VMEM), out_shape)
    return pl.pallas_call(
        kernel, out_shape=out_shape, in_specs=in_vmem(len(operands)), out_specs=outs, scratch_shapes=scratch,
        compiler_params=pltpu.CompilerParams(collective_id=number, has_side_effects=True),
    )(*operands)


def call(kernel, out_shape, operands, scratch):
    outs = jax.tree.map(lambda _: pl.BlockSpec(memory_space=pltpu.VMEM), out_shape)
    return pl.pallas_call(
        kernel, out_shape=out_shape,
        in_specs=[pl.BlockSpec(memory_space=pltpu.SMEM)] + in_vmem(len(operands) - 1),
        out_specs=outs, scratch_shapes=scratch,
    )(*operands)


def body(features, programs, column_pot, tile_pairs, pair_counts):
    feat, cells_blk = features.shape[1:]
    progs = programs.shape[1]
    tiles_blk = cells_blk // TILE
    most = tile_pairs.shape[2]
    blocks, n_sec = lax.axis_size("blk"), lax.axis_size("sec")
    tiles = tiles_blk * blocks
    width = TILE // blocks
    dims = (feat, blocks, tiles_blk, most)
    counts = (n_sec, blocks)
    f32, bf16 = jnp.float32, jnp.bfloat16
    shape = jax.ShapeDtypeStruct
    long = -(-(2 * most + 1) // 128) * 128
    listed = jnp.concatenate([tile_pairs[0], tile_pairs[1], pair_counts], axis=1)
    listed = jnp.pad(listed, ((0, 0), (0, long - listed.shape[1])))
    dma = pltpu.SemaphoreType.DMA
    mate_copies = (blocks - 1) * (tiles_blk + 2)

    own, xs, progs_all, pot, lists_all, lists = exchange(
        functools.partial(gather_kernel, counts), 0,
        (
            shape((blocks, tiles_blk, feat, width), bf16),
            shape((2, blocks, feat, cells_blk), bf16),
            shape((2, blocks, progs, cells_blk), bf16),
            shape((blocks, 1, cells_blk), bf16),
            shape((2, blocks, 1, long), jnp.int32),
            shape((blocks, 1, long), jnp.int32),
        ),
        (features[0], programs[0], column_pot, listed),
        [dma((STAGES * 5,)), dma((STAGES * 5,)), dma((mate_copies,)), dma((mate_copies,))],
    )

    xrec = pltpu.VMEM((tiles, 2 * HALF, width), bf16)
    yrec = pltpu.VMEM(((tiles + 1) * TILE, 2 * HALF), bf16)
    build = pltpu.VMEM((2 * HALF, TILE), f32)
    ext = pltpu.VMEM((tiles + 1, EXT, TILE), bf16)
    stat = pltpu.VMEM((tiles, 1, width), f32)
    acc = pltpu.VMEM((tiles, EXT, width), f32)
    index = pltpu.SMEM((blocks * most + UNROLL,), jnp.int32)
    pots = shape((blocks, tiles_blk, width), f32)
    all_pots = shape((blocks, blocks, tiles_blk, width), f32)
    sums = shape((tiles, EXT, width), f32)
    shift_scratch = [dma((blocks,)), dma((blocks,))]

    row_own = call(
        functools.partial(row_kernel, dims), pots, (lists, own, xs, pot),
        [xrec, yrec, build, stat, stat, index, index],
    )
    row_prev = exchange(functools.partial(shift_kernel, counts, 1), 1, all_pots, (row_own,), shift_scratch)
    col_own, back = call(
        functools.partial(col_kernel, dims), (pots, sums), (lists_all, own, xs, row_prev, progs_all),
        [xrec, yrec, build, ext, stat, stat, acc, index, index],
    )
    col_all = exchange(functools.partial(shift_kernel, counts, -1), 2, all_pots, (col_own,), shift_scratch)
    smooth = call(
        functools.partial(plan_kernel, dims),
        shape((blocks, tiles_blk, progs, width), bf16),
        (lists, own, xs, row_own, col_all, progs_all, back),
        [xrec, yrec, build, ext, acc, index, index],
    )
    return_copies = (blocks - 1) * (tiles_blk + 1)
    smoothed, row_out, col_out = exchange(
        functools.partial(return_kernel, counts), 3,
        (shape((progs, cells_blk), bf16), shape((1, cells_blk), f32), shape((1, cells_blk), f32)),
        (smooth, row_own, col_all),
        [pltpu.VMEM((blocks, tiles_blk, width), f32), dma((return_copies,)), dma((return_copies,))],
    )
    return smoothed[None], row_out, col_out


def solution(mesh):
    in_specs = (
        P("sec", None, "blk"),
        P("sec", None, "blk"),
        P("sec", "blk"),
        P(None, "sec", "blk"),
        P("sec", "blk"),
    )
    out_specs = (P("sec", None, "blk"), P("sec", "blk"), P("sec", "blk"))
    return jax.shard_map(body, mesh=mesh, in_specs=in_specs, out_specs=out_specs, check_vma=False)
```

time: 153 us -> 103 us (0.67)
  blocking collectives: 66.7 us -> 0 us
  Pallas kernels: 31.3 us -> 96.1 us
  starting transfers between devices: 25.5 us -> 0 us
  waiting for transfers between devices: 19.9 us -> 0 us
    pallas_call x3 -> x7, Pallas kernels: 31.3 us -> 96.1 us  [the longest x4 62.9 us: exchange(): pl.pallas_call(kernel, out_shape=out_shape, in_specs=in_vmem(len(operands...]
    all_gather x8 -> x0, blocking collectives: 61.8 us -> none  [the longest x2 15.4 us: body(): prog_next, prog_prev = (gather(prog_next), gather(prog_prev))]
    ppermute x7 -> x0, starting transfers between devices: 22.2 us -> none  [passed_along(): lax.ppermute(value, 'sec', [(source, source + steps) for source in range(...]
    ppermute x7 -> x0, waiting for transfers between devices: 16.7 us -> none  [passed_along(): lax.ppermute(value, 'sec', [(source, source + steps) for source in range(...]
    unnamed x1 -> x0, blocking collectives: 4.93 us -> none
    all_to_all x1 -> x0, starting transfers between devices: 3.33 us -> none  [body(): lax.all_to_all(smooth.reshape(blocks, tiles_blk, progs, width), 'blk', 0, 0)]
    all_to_all x1 -> x0, waiting for transfers between devices: 3.23 us -> none  [body(): lax.all_to_all(smooth.reshape(blocks, tiles_blk, progs, width), 'blk', 0, 0)]
    transpose x5 -> x0, local copies, waits for them, and re-layouts: 2.05 us -> none  [the longest x4 1.95 us: own_part(): return mine.transpose(1, 0, 2).reshape(1, cells_blk)]
  transfers between devices with their start and end apart: 8 -> 0, of which waited for: 2 -> 0; matrix products, arithmetic and copies ran while one was open for 2% -> 0% of each run, Pallas kernels for 6% -> 0%
where the time goes in v2:
time: 103 us
  Pallas kernels  96.1 us (93%)
  local copies, waits for them, and re-layouts  5.35 us (5%)
  between operations  1.31 us (1%)
    pallas_call x4, Pallas kernels, exchange(): pl.pallas_call(kernel, out_shape=out_shape, in_specs=in_vmem(len(operands...  62.9 us
    pallas_call x3, Pallas kernels, call(): pl.pallas_call(kernel, out_shape=out_shape, in_specs=[pl.BlockSpec(memory...  33.2 us
    unnamed x3, local copies, waits for them, and re-layouts  4.16 us

profile of v2, /device:TPU:0, one launch (start us, length us, event | category | flops | bytes accessed | tf_op | source)
XLA Modules:
  0.0 102.8 jit_solution(9187445293065514264)
XLA Ops:
  1.3 0.7 slice_bitcast_fusion.1
  2.0 0.1 pad_add_fusion
  2.0 0.5 pad.4.list_ref
  2.5 22.4 %shard_map.76 = (bf16[4,4,52,128]{3,2,1,0:T(8,128)(2,1)}, bf16[2,4,52,2048]{3,2,1,0:T(8,128)(2,1)}, bf16[2,4,32,2048]{3,2,1,0:T(8,128)(2,1)}, bf16[4,1,2048]{2,1...) custom-call(bf16[52,2048]{1,0:T(8,128)(2,1)} %bitcast.7, bf16[32,2048]{1,0:T(8,128)(2,1)} %bitcast.8, ...), custom_call_target="tpu_custom_call" | custom-call | tf_op jit(solution)/shard_map/pallas_call | solution.py:489
  24.9 10.4 %shard_map.77.part_ref.rp_ref.row_ref = f32[4,4,128]{2,1,0:T(4,128)} custom-call(s32[4,1,128]{2,1,0:T(1,128)} %get-tuple-element.14.lists_ref, bf16[4,4,52,128]{3,2,1,0:T(8,128)(2,1)} %get-tuple-element.15.own_ref, bf16[2,4,52,2048]{3,2,1,0:T(8,128)(2,1)} %get-tuple-element.16.next_ref.prev_ref, bf16[4,1,2048]{2,1,0:T(2,128)(2,1)} %get-tuple-element.17.pot_ref), custom_call_target="tpu_custom_call" | custom-call | tf_op jit(solution)/shard_map/pallas_call | solution.py:497
  35.3 11.2 %shard_map.78.rp_ref = f32[4,4,4,128]{3,2,1,0:T(4,128)} custom-call(f32[4,4,128]{2,1,0:T(4,128)} %shard_map.77.part_ref.rp_ref.row_ref), custom_call_target="tpu_custom_call" | custom-call | tf_op jit(solution)/shard_map/pallas_call | solution.py:489
  46.4 5.4 %shard_map.79 = (f32[4,4,128]{2,1,0:T(4,128)}, f32[16,48,128]{2,1,0:T(8,128)}) custom-call(s32[2,4,1,128]{3,2,1,0:T(1,128)} %get-tuple-element.18.lists_ref, bf16[4,4,52,128]{3,2,1,0:T(8,128)(2,1)} %get-tuple-element.15.own_ref, bf16[2,4,52,2048]{3,2,1,0:T(8,128)(2,1)} %get-tuple-element.16.next_ref.prev_ref, f32[4,4,4,128]{3,2,1,0:T(4,128)} %shard_map.78.rp_ref, ...), custom_call_target="tpu_custom_call" | custom-call | tf_op jit(solution)/shard_map/pallas_call | solution.py:497
  51.8 23.4 %shard_map.80.cp_ref.col_ref = f32[4,4,4,128]{3,2,1,0:T(4,128)} custom-call(f32[4,4,128]{2,1,0:T(4,128)} %get-tuple-element.20.part_ref), custom_call_target="tpu_custom_call" | custom-call | tf_op jit(solution)/shard_map/pallas_call | solution.py:489
  75.3 17.4 %shard_map.81.smooth_ref = bf16[4,4,32,128]{3,2,1,0:T(8,128)(2,1)} custom-call(s32[4,1,128]{2,1,0:T(1,128)} %get-tuple-element.14.lists_ref, bf16[4,4,52,128]{3,2,1,0:T(8,128)(2,1)} %get-tuple-element.15.own_ref, bf16[2,4,52,2048]{3,2,1,0:T(8,128)(2,1)} %get-tuple-element.16.next_ref.prev_ref, f32[4,4,128]{2,1,0:T(4,128)} %shard_map.77.part_ref.rp_ref.row_ref, ...), custom_call_target="tpu_custom_call" | custom-call | tf_op jit(solution)/shard_map/pallas_call | solution.py:497
  92.7 6.0 %shard_map.82 = (bf16[32,2048]{1,0:T(8,128)(2,1)}, f32[1,2048]{1,0:T(1,128)}, f32[1,2048]{1,0:T(1,128)}) custom-call(bf16[4,4,32,128]{3,2,1,0:T(8,128)(2,1)} %shard_map.81.smooth_ref, f32[4,4,128]{2,1,0:T(4,128)} %shard_map.77.part_ref.rp_ref.row_ref, f32[4,4,4,128]{3,2,1,0:T(4,128)} %shard_map.80.cp_ref.col_ref), custom_call_target="tpu_custom_call" | custom-call | tf_op jit(solution)/shard_map/pallas_call | solution.py:489
  98.7 1.6 %copy.12 = bf16[1,32,2048]{2,1,0:T(8,128)(2,1)} copy(bf16[1,32,2048]{2,1,0:T(8,128)(2,1)} %bitcast.9) | data formatting | bytes 262144
  100.3 1.3 %copy.13 = f32[1,2048]{1,0:T(1,128)} copy(f32[1,2048]{1,0:T(1,128)} %get-tuple-element.31) | data formatting | bytes 16384
  101.6 1.3 %copy.14 = f32[1,2048]{1,0:T(1,128)} copy(f32[1,2048]{1,0:T(1,128)} %get-tuple-element.32) | data formatting | bytes 16384

commit v3 on v2

--- a/solution.py
+++ b/solution.py
@@ -13,7 +13,8 @@
 LOG2E = math.log2(math.e)
 LN2 = math.log(2.0)
 NEG = -1e30
-UNROLL = 4
+UNROLL = 2
+SPLITS = 2
 HALF = 64
 EXT = 48
 
@@ -38,7 +39,7 @@
 
 
 def own_records(own_ref, xrec, feat, tiles_blk, tiles, bias_of):
-    width = TILE // (tiles // tiles_blk)
+    width = TILE // SPLITS
     gain = 2.0 * LOG2E / (feat * EPSILON)
     xrec[...] = jnp.zeros_like(xrec)
 
@@ -93,13 +94,17 @@
 
 
 def listed_pairs(lists_ref, mine, other, most, blocks, tiles_blk, tiles, own_first, used=True):
+    kinds = blocks // SPLITS
+    kind = lax.axis_index("blk") // SPLITS
+
     def of_block(block, place):
         def one(slot, at):
             row = lists_ref[block, 0, slot] + block * tiles_blk
             col = lists_ref[block, 0, most + slot]
-            mine[at] = row if own_first else col
-            other[at] = col if own_first else row
-            return at + 1
+            held, across = (row, col) if own_first else (col, row)
+            mine[at] = held // kinds
+            other[at] = across
+            return at + jnp.where(held % kinds == kind, 1, 0)
 
         return lax.fori_loop(0, jnp.where(used, lists_ref[block, 0, 2 * most], 0), one, place)
 
@@ -117,7 +122,10 @@
 
 
 def spread(parts_ref, tile, blocks, tiles_blk):
-    parts = [parts_ref[block, tile // tiles_blk, pl.ds(tile % tiles_blk, 1), :] for block in range(blocks)]
+    kinds = blocks // SPLITS
+    first = (tile % kinds) * SPLITS
+    place = (tile % tiles_blk) // kinds
+    parts = [parts_ref[first + n, tile // tiles_blk, pl.ds(place, 1), :] for n in range(SPLITS)]
     return jnp.concatenate(parts, axis=1)
 
 
@@ -126,13 +134,20 @@
     return odd if forward else 1 - odd
 
 
+def lane_of(owner, place, blocks):
+    kinds = blocks // SPLITS
+    return (place * kinds + owner // SPLITS) * TILE + (owner % SPLITS) * (TILE // SPLITS)
+
+
 def row_kernel(dims, lists_ref, own_ref, next_ref, pot_ref, rp_ref, xrec, yrec, build, high, total, mine, other):
     feat, blocks, tiles_blk, most = dims
     tiles = blocks * tiles_blk
+    held_blk = tiles_blk * SPLITS // blocks
+    held = blocks * held_blk
     to_score = LOG2E / EPSILON
     groups = listed_pairs(lists_ref, mine, other, most, blocks, tiles_blk, tiles, True)
     own_records(
-        own_ref, xrec, feat, tiles_blk, tiles,
+        own_ref, xrec, feat, held_blk, held,
         lambda tile, cells: jnp.zeros((1, cells.shape[1]), jnp.float32),
     )
 
@@ -158,16 +173,18 @@
 
     lax.fori_loop(0, groups, group, 0)
     at_end = lax.axis_index("sec") == lax.axis_size("sec") - 1
-    for tile in range(tiles):
-        cells = own_ref[tile // tiles_blk, tile % tiles_blk].astype(jnp.float32)
+    for tile in range(held):
+        cells = own_ref[tile // held_blk, tile % held_blk].astype(jnp.float32)
         score = high[tile] + jnp.log2(total[tile]) - sum_squares(cells) * (to_score / feat)
-        rp_ref[tile // tiles_blk, tile % tiles_blk : tile % tiles_blk + 1, :] = jnp.where(at_end, 0.0, score * (-EPSILON * LN2))
+        rp_ref[tile // held_blk, tile % held_blk : tile % held_blk + 1, :] = jnp.where(at_end, 0.0, score * (-EPSILON * LN2))
 
 
 def col_kernel(dims, lists_ref, own_ref, prev_ref, rp_ref, prog_ref, cp_ref, back_ref,
                xrec, yrec, build, ext, high, total, acc, mine, other):
     feat, blocks, tiles_blk, most = dims
     tiles = blocks * tiles_blk
+    held_blk = tiles_blk * SPLITS // blocks
+    held = blocks * held_blk
     to_score = LOG2E / EPSILON
     progs = prog_ref.shape[2]
     used = lax.axis_index("sec") > 0
@@ -175,7 +192,7 @@
         lists_ref.at[near_side(False)], mine, other, most, blocks, tiles_blk, tiles, False, used
     )
     own_records(
-        own_ref, xrec, feat, tiles_blk, tiles,
+        own_ref, xrec, feat, held_blk, held,
         lambda tile, cells: jnp.zeros((1, cells.shape[1]), jnp.float32),
     )
 
@@ -205,24 +222,26 @@
         return carry
 
     lax.fori_loop(0, groups, group, 0)
-    for tile in range(tiles):
-        cells = own_ref[tile // tiles_blk, tile % tiles_blk].astype(jnp.float32)
+    for tile in range(held):
+        cells = own_ref[tile // held_blk, tile % held_blk].astype(jnp.float32)
         filled = total[tile] > 0.0
         score = high[tile] + jnp.log2(total[tile]) - sum_squares(cells) * (to_score / feat)
-        cp_ref[tile // tiles_blk, tile % tiles_blk : tile % tiles_blk + 1, :] = jnp.where(filled, score * (-EPSILON * LN2), 0.0)
+        cp_ref[tile // held_blk, tile % held_blk : tile % held_blk + 1, :] = jnp.where(filled, score * (-EPSILON * LN2), 0.0)
         back_ref[tile] = jnp.where(filled, acc[tile] / total[tile], 0.0)
 
 
-def plan_kernel(dims, lists_ref, own_ref, next_ref, rp_ref, cp_ref, prog_ref, back_ref, out_ref,
+def plan_kernel(dims, lists_ref, own_ref, next_ref, rp_ref, cp_ref, prog_ref, back_ref, home_ref, out_ref, rows_ref, cols_ref,
                 xrec, yrec, build, ext, acc, mine, other):
     feat, blocks, tiles_blk, most = dims
     tiles = blocks * tiles_blk
+    held_blk = tiles_blk * SPLITS // blocks
+    held = blocks * held_blk
     to_score = LOG2E / EPSILON
     progs = prog_ref.shape[2]
     groups = listed_pairs(lists_ref, mine, other, most, blocks, tiles_blk, tiles, True)
     own_records(
-        own_ref, xrec, feat, tiles_blk, tiles,
-        lambda tile, cells: (rp_ref[tile // tiles_blk, pl.ds(tile % tiles_blk, 1), :] - sum_squares(cells) / feat) * to_score,
+        own_ref, xrec, feat, held_blk, held,
+        lambda tile, cells: (rp_ref[tile // held_blk, pl.ds(tile % held_blk, 1), :] - sum_squares(cells) / feat) * to_score,
     )
 
     def bias(tile, start, cells):
@@ -231,6 +250,12 @@
     other_records(next_ref.at[near_side(True)], yrec, build, feat, tiles_blk, tiles, bias)
     ext_records(prog_ref.at[near_side(True)], ext, progs, tiles_blk, tiles)
     acc[...] = back_ref[...]
+    width = TILE // SPLITS
+    for owner in range(blocks):
+        for place in range(held_blk):
+            start = lane_of(owner, place, blocks)
+            rows_ref[:, start : start + width] = home_ref[owner, place : place + 1, :]
+            cols_ref[:, start : start + width] = cp_ref[owner, lax.axis_index("blk"), place : place + 1, :]
 
     def group(index, carry):
         for step in range(UNROLL):
@@ -241,9 +266,9 @@
         return carry
 
     lax.fori_loop(0, groups, group, 0)
-    for tile in range(tiles):
+    for tile in range(held):
         sums = acc[tile]
-        out_ref[tile // tiles_blk, tile % tiles_blk] = (sums[0:progs] / sums[progs : progs + 1]).astype(jnp.bfloat16)
+        out_ref[tile // held_blk, tile % held_blk] = (sums[0:progs] / sums[progs : progs + 1]).astype(jnp.bfloat16)
 
 
 MESH = pl.DeviceIdType.MESH
@@ -292,8 +317,8 @@
         + [(yes, sec, mate) for mate in mates]
     )
     sems, mate_sems = (send_sem, recv_sem), (mate_send, mate_recv)
-    width = TILE // blocks
-    tiles_blk = x_ref.shape[1] // TILE
+    width = TILE // SPLITS
+    held_blk = x_ref.shape[1] // TILE * SPLITS // blocks
     half = x_ref.shape[1] // 2
     sources = [
         (list_ref, lists_ref, None), (x_ref, xs_ref, 0), (x_ref, xs_ref, 1), (prog_ref, progs_ref, 0), (prog_ref, progs_ref, 1),
@@ -324,8 +349,8 @@
     def to_mate(k):
         mate = mates[k]
         copies = []
-        for tile in range(tiles_blk):
-            start = pl.multiple_of(tile * TILE + mate * width, width)
+        for tile in range(held_blk):
+            start = pl.multiple_of(lane_of(mate, tile, blocks), width)
             copies.append((x_ref.at[:, pl.ds(start, width)], own_ref.at[blk, tile]))
         copies.append((pot_ref, pots_ref.at[blk]))
         copies.append((list_ref, all_lists_ref.at[blk]))
@@ -338,8 +363,8 @@
     for k in range(3):
         for copy in to_mate(k):
             copy.start()
-    for tile in range(tiles_blk):
-        start = pl.multiple_of(tile * TILE + blk * width, width)
+    for tile in range(held_blk):
+        start = pl.multiple_of(lane_of(blk, tile, blocks), width)
         own_ref[blk, tile] = x_ref[:, pl.ds(start, width)]
     pots_ref[blk] = pot_ref[...]
     all_lists_ref[blk] = list_ref[...]
@@ -402,17 +427,24 @@
             copy.wait_send()
 
 
-def shift_kernel(counts, steps, part_ref, out_ref, send_sem, recv_sem):
+def shift_kernel(counts, steps, home, part_ref, out_ref, *rest):
+    home_ref = rest[0] if home else None
+    send_sem, recv_sem = rest[-2:]
     n_sec, blocks = counts
     sec, blk = lax.axis_index("sec"), lax.axis_index("blk")
     to, source = sec + steps, sec - steps
     has_to = jnp.logical_and(to >= 0, to < n_sec)
     has_from = jnp.logical_and(source >= 0, source < n_sec)
     targets = [(blk + turn) % blocks for turn in range(blocks)]
-    greet([(has_to, to, mate) for mate in targets] + [(has_from, source, mate) for mate in targets])
+    mates = [(sec >= 0, sec, mate) for mate in targets[1:]] if home else []
+    greet(mates + [(has_to, to, mate) for mate in targets] + [(has_from, source, mate) for mate in targets])
 
     def copy(turn):
         return send(part_ref, out_ref.at[blk], (send_sem, recv_sem), turn, to, targets[turn])
+
+    def homeward(turn, owner):
+        src = part_ref.at[targets[turn]]
+        return send(src, home_ref.at[owner], (send_sem, recv_sem), blocks + turn - 1, sec, targets[turn])
 
     def arrival(turn):
         slot = out_ref.at[(blk + blocks - turn) % blocks]
@@ -423,6 +455,13 @@
         for turn in range(blocks):
             copy(turn).start()
 
+    if home:
+        for turn in range(1, blocks):
+            homeward(turn, blk).start()
+        home_ref[blk] = part_ref[blk]
+        for turn in range(1, blocks):
+            homeward(turn, (blk + blocks - turn) % blocks).wait_recv()
+
     @pl.when(has_from)
     def _():
         for turn in range(blocks):
@@ -437,46 +476,37 @@
         for turn in range(blocks):
             copy(turn).wait_send()
 
-
-def return_kernel(counts, smooth_ref, row_ref, col_ref, out_ref, rows_ref, cols_ref, parts, send_sem, recv_sem):
+    if home:
+        for turn in range(1, blocks):
+            homeward(turn, blk).wait_send()
+
+
+def return_kernel(counts, smooth_ref, out_ref, send_sem, recv_sem):
     n_sec, blocks = counts
     sec, blk = lax.axis_index("sec"), lax.axis_index("blk")
-    tiles_blk, width = row_ref.shape[1:]
+    held_blk, width = smooth_ref.shape[1], smooth_ref.shape[3]
     mates = [(blk + turn) % blocks for turn in range(blocks)]
     greet([(sec >= 0, sec, mate) for mate in mates[1:]])
-    sems = (send_sem, recv_sem)
-    per = tiles_blk + 1
-
-    def copies(turn, arriving):
-        mate = mates[turn]
-        owner = (blk + blocks - turn) % blocks if arriving else blk
-        pairs = []
-        for tile in range(tiles_blk):
-            start = pl.multiple_of(tile * TILE + owner * width, width)
-            pairs.append((smooth_ref.at[mate, tile], out_ref.at[:, pl.ds(start, width)]))
-        pairs.append((row_ref.at[mate], parts.at[owner]))
-        return [send(src, dst, sems, per * (turn - 1) + n, sec, mate) for n, (src, dst) in enumerate(pairs)]
+
+    def copies(turn, owner):
+        found = []
+        for place in range(held_blk):
+            start = pl.multiple_of(lane_of(owner, place, blocks), width)
+            src, dst = smooth_ref.at[mates[turn], place], out_ref.at[:, pl.ds(start, width)]
+            found.append(send(src, dst, (send_sem, recv_sem), held_blk * (turn - 1) + place, sec, mates[turn]))
+        return found
 
     for turn in range(1, blocks):
-        for copy in copies(turn, False):
+        for copy in copies(turn, blk):
             copy.start()
-    for tile in range(tiles_blk):
-        start = pl.multiple_of(tile * TILE + blk * width, width)
-        out_ref[:, pl.ds(start, width)] = smooth_ref[blk, tile]
-    parts[blk] = row_ref[blk]
-    for owner in range(blocks):
-        for tile in range(tiles_blk):
-            start = tile * TILE + owner * width
-            cols_ref[:, start : start + width] = col_ref[owner, blk, tile : tile + 1, :]
+    for place in range(held_blk):
+        start = pl.multiple_of(lane_of(blk, place, blocks), width)
+        out_ref[:, pl.ds(start, width)] = smooth_ref[blk, place]
     for turn in range(1, blocks):
-        for copy in copies(turn, True):
+        for copy in copies(turn, (blk + blocks - turn) % blocks):
             copy.wait_recv()
-    for owner in range(blocks):
-        for tile in range(tiles_blk):
-            start = tile * TILE + owner * width
-            rows_ref[:, start : start + width] = parts[owner, tile : tile + 1, :]
     for turn in range(1, blocks):
-        for copy in copies(turn, False):
+        for copy in copies(turn, blk):
             copy.wait_send()
 
 
@@ -508,7 +538,9 @@
     most = tile_pairs.shape[2]
     blocks, n_sec = lax.axis_size("blk"), lax.axis_size("sec")
     tiles = tiles_blk * blocks
-    width = TILE // blocks
+    width = TILE // SPLITS
+    held_blk = tiles_blk * SPLITS // blocks
+    held = blocks * held_blk
     dims = (feat, blocks, tiles_blk, most)
     counts = (n_sec, blocks)
     f32, bf16 = jnp.float32, jnp.bfloat16
@@ -517,12 +549,12 @@
     listed = jnp.concatenate([tile_pairs[0], tile_pairs[1], pair_counts], axis=1)
     listed = jnp.pad(listed, ((0, 0), (0, long - listed.shape[1])))
     dma = pltpu.SemaphoreType.DMA
-    mate_copies = (blocks - 1) * (tiles_blk + 2)
+    mate_copies = (blocks - 1) * (held_blk + 2)
 
     own, xs, progs_all, pot, lists_all, lists = exchange(
         functools.partial(gather_kernel, counts), 0,
         (
-            shape((blocks, tiles_blk, feat, width), bf16),
+            shape((blocks, held_blk, feat, width), bf16),
             shape((2, blocks, feat, cells_blk), bf16),
             shape((2, blocks, progs, cells_blk), bf16),
             shape((blocks, 1, cells_blk), bf16),
@@ -533,40 +565,43 @@
         [dma((STAGES * 5,)), dma((STAGES * 5,)), dma((mate_copies,)), dma((mate_copies,))],
     )
 
-    xrec = pltpu.VMEM((tiles, 2 * HALF, width), bf16)
+    xrec = pltpu.VMEM((held, 2 * HALF, width), bf16)
     yrec = pltpu.VMEM(((tiles + 1) * TILE, 2 * HALF), bf16)
     build = pltpu.VMEM((2 * HALF, TILE), f32)
     ext = pltpu.VMEM((tiles + 1, EXT, TILE), bf16)
-    stat = pltpu.VMEM((tiles, 1, width), f32)
-    acc = pltpu.VMEM((tiles, EXT, width), f32)
+    stat = pltpu.VMEM((held, 1, width), f32)
+    acc = pltpu.VMEM((held, EXT, width), f32)
     index = pltpu.SMEM((blocks * most + UNROLL,), jnp.int32)
-    pots = shape((blocks, tiles_blk, width), f32)
-    all_pots = shape((blocks, blocks, tiles_blk, width), f32)
-    sums = shape((tiles, EXT, width), f32)
-    shift_scratch = [dma((blocks,)), dma((blocks,))]
+    pots = shape((blocks, held_blk, width), f32)
+    all_pots = shape((blocks, blocks, held_blk, width), f32)
+    sums = shape((held, EXT, width), f32)
 
     row_own = call(
         functools.partial(row_kernel, dims), pots, (lists, own, xs, pot),
         [xrec, yrec, build, stat, stat, index, index],
     )
-    row_prev = exchange(functools.partial(shift_kernel, counts, 1), 1, all_pots, (row_own,), shift_scratch)
+    row_prev, row_home = exchange(
+        functools.partial(shift_kernel, counts, 1, True), 1, (all_pots, pots), (row_own,),
+        [dma((2 * blocks - 1,)), dma((2 * blocks - 1,))],
+    )
     col_own, back = call(
         functools.partial(col_kernel, dims), (pots, sums), (lists_all, own, xs, row_prev, progs_all),
         [xrec, yrec, build, ext, stat, stat, acc, index, index],
     )
-    col_all = exchange(functools.partial(shift_kernel, counts, -1), 2, all_pots, (col_own,), shift_scratch)
-    smooth = call(
+    col_all = exchange(
+        functools.partial(shift_kernel, counts, -1, False), 2, all_pots, (col_own,), [dma((blocks,)), dma((blocks,))]
+    )
+    line = shape((1, cells_blk), f32)
+    smooth, row_out, col_out = call(
         functools.partial(plan_kernel, dims),
-        shape((blocks, tiles_blk, progs, width), bf16),
-        (lists, own, xs, row_own, col_all, progs_all, back),
+        (shape((blocks, held_blk, progs, width), bf16), line, line),
+        (lists, own, xs, row_own, col_all, progs_all, back, row_home),
         [xrec, yrec, build, ext, acc, index, index],
     )
-    return_copies = (blocks - 1) * (tiles_blk + 1)
-    smoothed, row_out, col_out = exchange(
-        functools.partial(return_kernel, counts), 3,
-        (shape((progs, cells_blk), bf16), shape((1, cells_blk), f32), shape((1, cells_blk), f32)),
-        (smooth, row_own, col_all),
-        [pltpu.VMEM((blocks, tiles_blk, width), f32), dma((return_copies,)), dma((return_copies,))],
+    return_copies = (blocks - 1) * held_blk
+    smoothed = exchange(
+        functools.partial(return_kernel, counts), 3, shape((progs, cells_blk), bf16), (smooth,),
+        [dma((return_copies,)), dma((return_copies,))],
     )
     return smoothed[None], row_out, col_out
 

time: 103 us -> 93.5 us (0.908)
  Pallas kernels: 96.1 us -> 89.1 us
  local copies, waits for them, and re-layouts: 5.35 us -> 2.76 us
    pallas_call x3, Pallas kernels: 33.2 us -> 29 us  [call(): pl.pallas_call(kernel, out_shape=out_shape, in_specs=[pl.BlockSpec(memory...]
    pallas_call x4, Pallas kernels: 62.9 us -> 60.1 us  [exchange(): pl.pallas_call(kernel, out_shape=out_shape, in_specs=in_vmem(len(operands...]
    unnamed x3 -> x1, local copies, waits for them, and re-layouts: 4.16 us -> 1.57 us
where the time goes in v3:
time: 93.5 us; the launch traced here: 93.2 us
  Pallas kernels  89.1 us (95%)
  local copies, waits for them, and re-layouts  2.76 us (3%)
  between operations  1.31 us (1%)
    pallas_call x4, Pallas kernels, exchange(): pl.pallas_call(kernel, out_shape=out_shape, in_specs=in_vmem(len(operands...  60.1 us
    pallas_call x3, Pallas kernels, call(): pl.pallas_call(kernel, out_shape=out_shape, in_specs=[pl.BlockSpec(memory...  29 us

profile of v3, /device:TPU:0, one launch (start us, length us, event | category | flops | bytes accessed | tf_op | source)
XLA Modules:
  0.0 93.2 jit_solution(2317596294243019805)
XLA Ops:
  1.3 0.7 slice_bitcast_fusion.1
  2.0 0.1 pad_add_fusion
  2.0 0.5 pad.4.list_ref
  2.5 22.3 %shard_map.76 = (bf16[4,2,52,256]{3,2,1,0:T(8,128)(2,1)}, bf16[2,4,52,2048]{3,2,1,0:T(8,128)(2,1)}, bf16[2,4,32,2048]{3,2,1,0:T(8,128)(2,1)}, bf16[4,1,2048]{2,1...) custom-call(bf16[52,2048]{1,0:T(8,128)(2,1)} %bitcast.8, bf16[32,2048]{1,0:T(8,128)(2,1)} %bitcast.9, ...), custom_call_target="tpu_custom_call" | custom-call | tf_op jit(solution)/shard_map/pallas_call | solution.py:519
  24.8 10.3 %shard_map.77.part_ref.rp_ref = f32[4,2,256]{2,1,0:T(2,128)} custom-call(s32[4,1,128]{2,1,0:T(1,128)} %get-tuple-element.16.lists_ref, bf16[4,2,52,256]{3,2,1,0:T(8,128)(2,1)} %get-tuple-element.17.own_ref, bf16[2,4,52,2048]{3,2,1,0:T(8,128)(2,1)} %get-tuple-element.18.next_ref.prev_ref, bf16[4,1,2048]{2,1,0:T(2,128)(2,1)} %get-tuple-element.19.pot_ref), custom_call_target="tpu_custom_call" | custom-call | tf_op jit(solution)/shard_map/pallas_call | solution.py:527
  35.1 12.8 %shard_map.78 = (f32[4,4,2,256]{3,2,1,0:T(2,128)}, f32[4,2,256]{2,1,0:T(2,128)}) custom-call(f32[4,2,256]{2,1,0:T(2,128)} %shard_map.77.part_ref.rp_ref), custom_call_target="tpu_custom_call" | custom-call | tf_op jit(solution)/shard_map/pallas_call | solution.py:519
  47.9 5.3 %shard_map.79 = (f32[4,2,256]{2,1,0:T(2,128)}, f32[8,48,256]{2,1,0:T(8,128)}) custom-call(s32[2,4,1,128]{3,2,1,0:T(1,128)} %get-tuple-element.20.lists_ref, bf16[4,2,52,256]{3,2,1,0:T(8,128)(2,1)} %get-tuple-element.17.own_ref, bf16[2,4,52,2048]{3,2,1,0:T(8,128)(2,1)} %get-tuple-element.18.next_ref.prev_ref, f32[4,4,2,256]{3,2,1,0:T(2,128)} %get-tuple-element.21.rp_ref, ...), custom_call_target="tpu_custom_call" | custom-call | tf_op jit(solution)/shard_map/pallas_call | solution.py:527
  53.2 19.3 %shard_map.80.cp_ref = f32[4,4,2,256]{3,2,1,0:T(2,128)} custom-call(f32[4,2,256]{2,1,0:T(2,128)} %get-tuple-element.23.part_ref), custom_call_target="tpu_custom_call" | custom-call | tf_op jit(solution)/shard_map/pallas_call | solution.py:519
  72.5 13.4 %shard_map.81 = (bf16[4,2,32,256]{3,2,1,0:T(8,128)(2,1)}, f32[1,2048]{1,0:T(1,128)}, f32[1,2048]{1,0:T(1,128)}) custom-call(s32[4,1,128]{2,1,0:T(1,128)} %get-tuple-element.16.lists_ref, bf16[4,2,52,256]{3,2,1,0:T(8,128)(2,1)} %get-tuple-element.17.own_ref, bf16[2,4,52,2048]{3,2,1,0:T(8,128)(2,1)} %get-tuple-element.18.next_ref.prev_ref, ...), custom_call_target="tpu_custom_call" | custom-call | tf_op jit(solution)/shard_map/pallas_call | solution.py:527
  85.9 5.7 %shard_map.82 = bf16[32,2048]{1,0:T(8,128)(2,1)} custom-call(bf16[4,2,32,256]{3,2,1,0:T(8,128)(2,1)} %get-tuple-element.26.smooth_ref), custom_call_target="tpu_custom_call" | custom-call | tf_op jit(solution)/shard_map/pallas_call | solution.py:519
  91.7 1.6 %copy.10 = bf16[1,32,2048]{2,1,0:T(8,128)(2,1)} copy(bf16[1,32,2048]{2,1,0:T(8,128)(2,1)} %bitcast.7) | data formatting | bytes 262144

commit v4 on v3

--- a/solution.py
+++ b/solution.py
@@ -109,8 +109,8 @@
         return lax.fori_loop(0, jnp.where(used, lists_ref[block, 0, 2 * most], 0), one, place)
 
     total = lax.fori_loop(0, blocks, of_block, 0)
-    last = mine[jnp.maximum(total - 1, 0)]
-    for extra in range(UNROLL - 1):
+    last = jnp.where(total > 0, mine[jnp.maximum(total - 1, 0)], 0)
+    for extra in range(2 * UNROLL):
         mine[total + extra] = last
         other[total + extra] = tiles
     return (total + UNROLL - 1) // UNROLL
@@ -119,6 +119,25 @@
 def scores_of(yrec, xrec, mine, other):
     rows = yrec[pl.ds(pl.multiple_of(other * TILE, TILE), TILE), :]
     return jnp.dot(rows, xrec[mine], preferred_element_type=jnp.float32)
+
+
+def over_pairs(groups, ready, tops, yrec, xrec, mine, other, use):
+    def make(at, place):
+        scores = scores_of(yrec, xrec, mine[at], other[at])
+        ready[place][...] = scores
+        if tops is not None:
+            tops[place] = jnp.max(scores, axis=0, keepdims=True)
+
+    make(0, 0)
+
+    def group(index, carry):
+        for step in range(UNROLL):
+            at = index * UNROLL + step
+            make(at + 1, (step + 1) % UNROLL)
+            use(ready[step], None if tops is None else tops[step], mine[at], other[at])
+        return carry
+
+    lax.fori_loop(0, groups, group, 0)
 
 
 def spread(parts_ref, tile, blocks, tiles_blk):
@@ -139,7 +158,7 @@
     return (place * kinds + owner // SPLITS) * TILE + (owner % SPLITS) * (TILE // SPLITS)
 
 
-def row_kernel(dims, lists_ref, own_ref, next_ref, pot_ref, rp_ref, xrec, yrec, build, high, total, mine, other):
+def row_kernel(dims, lists_ref, own_ref, next_ref, pot_ref, rp_ref, xrec, yrec, build, high, total, mine, other, *ready):
     feat, blocks, tiles_blk, most = dims
     tiles = blocks * tiles_blk
     held_blk = tiles_blk * SPLITS // blocks
@@ -159,19 +178,14 @@
     high[...] = jnp.full_like(high, NEG)
     total[...] = jnp.zeros_like(total)
 
-    def group(index, carry):
-        for step in range(UNROLL):
-            at = index * UNROLL + step
-            row = mine[at]
-            scores = scores_of(yrec, xrec, row, other[at])
-            old = high[row]
-            new = jnp.maximum(old, jnp.max(scores, axis=0, keepdims=True))
-            part = jnp.sum(jnp.exp2(scores - new), axis=0, keepdims=True)
-            total[row] = total[row] * jnp.exp2(old - new) + part
-            high[row] = new
-        return carry
-
-    lax.fori_loop(0, groups, group, 0)
+    def use(scores_ref, top, row, col):
+        old = high[row]
+        new = jnp.maximum(old, jnp.max(scores_ref[...], axis=0, keepdims=True))
+        part = jnp.sum(jnp.exp2(scores_ref[...] - new), axis=0, keepdims=True)
+        total[row] = total[row] * jnp.exp2(old - new) + part
+        high[row] = new
+
+    over_pairs(groups, ready, None, yrec, xrec, mine, other, use)
     at_end = lax.axis_index("sec") == lax.axis_size("sec") - 1
     for tile in range(held):
         cells = own_ref[tile // held_blk, tile % held_blk].astype(jnp.float32)
@@ -180,7 +194,7 @@
 
 
 def col_kernel(dims, lists_ref, own_ref, prev_ref, rp_ref, prog_ref, cp_ref, back_ref,
-               xrec, yrec, build, ext, high, total, acc, mine, other):
+               xrec, yrec, build, ext, high, total, acc, mine, other, tops, *ready):
     feat, blocks, tiles_blk, most = dims
     tiles = blocks * tiles_blk
     held_blk = tiles_blk * SPLITS // blocks
@@ -205,23 +219,18 @@
     total[...] = jnp.zeros_like(total)
     acc[...] = jnp.zeros_like(acc)
 
-    def group(index, carry):
-        for step in range(UNROLL):
-            at = index * UNROLL + step
-            col, row = mine[at], other[at]
-            scores = scores_of(yrec, xrec, col, row)
-            old = high[col]
-            new = jnp.maximum(old, jnp.max(scores, axis=0, keepdims=True))
-            weight = jnp.exp2(scores - new)
-            part = jnp.sum(weight, axis=0, keepdims=True)
-            shrink = jnp.exp2(old - new)
-            sums = jnp.dot(ext[row], weight.astype(jnp.bfloat16), preferred_element_type=jnp.float32)
-            acc[col] = acc[col] * shrink + sums
-            total[col] = total[col] * shrink + part
-            high[col] = new
-        return carry
-
-    lax.fori_loop(0, groups, group, 0)
+    def use(scores_ref, top, col, row):
+        old = high[col]
+        new = jnp.maximum(old, top)
+        weight = jnp.exp2(scores_ref[...] - new)
+        part = jnp.sum(weight, axis=0, keepdims=True)
+        shrink = jnp.exp2(old - new)
+        sums = jnp.dot(ext[row], weight.astype(jnp.bfloat16), preferred_element_type=jnp.float32)
+        acc[col] = acc[col] * shrink + sums
+        total[col] = total[col] * shrink + part
+        high[col] = new
+
+    over_pairs(groups, ready, tops, yrec, xrec, mine, other, use)
     for tile in range(held):
         cells = own_ref[tile // held_blk, tile % held_blk].astype(jnp.float32)
         filled = total[tile] > 0.0
@@ -231,7 +240,7 @@
 
 
 def plan_kernel(dims, lists_ref, own_ref, next_ref, rp_ref, cp_ref, prog_ref, back_ref, home_ref, out_ref, rows_ref, cols_ref,
-                xrec, yrec, build, ext, acc, mine, other):
+                xrec, yrec, build, ext, acc, mine, other, *ready):
     feat, blocks, tiles_blk, most = dims
     tiles = blocks * tiles_blk
     held_blk = tiles_blk * SPLITS // blocks
@@ -257,15 +266,11 @@
             rows_ref[:, start : start + width] = home_ref[owner, place : place + 1, :]
             cols_ref[:, start : start + width] = cp_ref[owner, lax.axis_index("blk"), place : place + 1, :]
 
-    def group(index, carry):
-        for step in range(UNROLL):
-            at = index * UNROLL + step
-            row, col = mine[at], other[at]
-            plan = jnp.exp2(scores_of(yrec, xrec, row, col)).astype(jnp.bfloat16)
-            acc[row] = acc[row] + jnp.dot(ext[col], plan, preferred_element_type=jnp.float32)
-        return carry
-
-    lax.fori_loop(0, groups, group, 0)
+    def use(scores_ref, top, row, col):
+        plan = jnp.exp2(scores_ref[...]).astype(jnp.bfloat16)
+        acc[row] = acc[row] + jnp.dot(ext[col], plan, preferred_element_type=jnp.float32)
+
+    over_pairs(groups, ready, None, yrec, xrec, mine, other, use)
     for tile in range(held):
         sums = acc[tile]
         out_ref[tile // held_blk, tile % held_blk] = (sums[0:progs] / sums[progs : progs + 1]).astype(jnp.bfloat16)
@@ -368,30 +373,32 @@
         own_ref[blk, tile] = x_ref[:, pl.ds(start, width)]
     pots_ref[blk] = pot_ref[...]
     all_lists_ref[blk] = list_ref[...]
-    for c in chunks:
-        first(c).wait_recv()
-
-        @pl.when(has_to)
-        def _():
-            relay(c).start()
-
-        share(c, 0, 0).start()
-        share(c, 0, 1).start()
-    for c in chunks:
-        share(c, 0, 0).wait_recv()
-        share(c, 0, 2).start()
-
-        @pl.when(has_from)
-        def _():
-            relay(c).wait_recv()
-            share(c, 1, 0).start()
-            share(c, 1, 1).start()
-
-    @pl.when(has_from)
-    def _():
-        for c in chunks:
-            share(c, 1, 0).wait_recv()
-            share(c, 1, 2).start()
+    for turn in range(len(sources) + 2):
+        if turn in chunks:
+            first(turn).wait_recv()
+
+            @pl.when(has_to)
+            def _():
+                relay(turn).start()
+
+            share(turn, 0, 0).start()
+            share(turn, 0, 1).start()
+        if turn - 1 in chunks:
+            share(turn - 1, 0, 0).wait_recv()
+            share(turn - 1, 0, 2).start()
+
+            @pl.when(has_from)
+            def _():
+                relay(turn - 1).wait_recv()
+                share(turn - 1, 1, 0).start()
+                share(turn - 1, 1, 1).start()
+
+        if turn - 2 in chunks:
+
+            @pl.when(has_from)
+            def _():
+                share(turn - 2, 1, 0).wait_recv()
+                share(turn - 2, 1, 2).start()
 
     for c in chunks:
         for kind in (1, 2):
@@ -571,14 +578,16 @@
     ext = pltpu.VMEM((tiles + 1, EXT, TILE), bf16)
     stat = pltpu.VMEM((held, 1, width), f32)
     acc = pltpu.VMEM((held, EXT, width), f32)
-    index = pltpu.SMEM((blocks * most + UNROLL,), jnp.int32)
+    index = pltpu.SMEM((blocks * most + 2 * UNROLL,), jnp.int32)
+    ready = [pltpu.VMEM((TILE, width), f32)] * UNROLL
+    tops = pltpu.VMEM((UNROLL, 1, width), f32)
     pots = shape((blocks, held_blk, width), f32)
     all_pots = shape((blocks, blocks, held_blk, width), f32)
     sums = shape((held, EXT, width), f32)
 
     row_own = call(
         functools.partial(row_kernel, dims), pots, (lists, own, xs, pot),
-        [xrec, yrec, build, stat, stat, index, index],
+        [xrec, yrec, build, stat, stat, index, index, *ready],
     )
     row_prev, row_home = exchange(
         functools.partial(shift_kernel, counts, 1, True), 1, (all_pots, pots), (row_own,),
@@ -586,7 +595,7 @@
     )
     col_own, back = call(
         functools.partial(col_kernel, dims), (pots, sums), (lists_all, own, xs, row_prev, progs_all),
-        [xrec, yrec, build, ext, stat, stat, acc, index, index],
+        [xrec, yrec, build, ext, stat, stat, acc, index, index, tops, *ready],
     )
     col_all = exchange(
         functools.partial(shift_kernel, counts, -1, False), 2, all_pots, (col_own,), [dma((blocks,)), dma((blocks,))]
@@ -596,7 +605,7 @@
         functools.partial(plan_kernel, dims),
         (shape((blocks, held_blk, progs, width), bf16), line, line),
         (lists, own, xs, row_own, col_all, progs_all, back, row_home),
-        [xrec, yrec, build, ext, acc, index, index],
+        [xrec, yrec, build, ext, acc, index, index, *ready],
     )
     return_copies = (blocks - 1) * held_blk
     smoothed = exchange(

time: 93.5 us -> 89 us (0.952)
  Pallas kernels: 89.1 us -> 84.6 us
    pallas_call x3, Pallas kernels: 29 us -> 26 us  [call(): pl.pallas_call(kernel, out_shape=out_shape, in_specs=[pl.BlockSpec(memory...]
    pallas_call x4, Pallas kernels: 60.1 us -> 58.6 us  [exchange(): pl.pallas_call(kernel, out_shape=out_shape, in_specs=in_vmem(len(operands...]
where the time goes in v4:
time: 89 us; the launch traced here: 88.7 us
  Pallas kernels  84.6 us (95%)
  local copies, waits for them, and re-layouts  2.76 us (3%)
  between operations  1.31 us (1%)
    pallas_call x4, Pallas kernels, exchange(): pl.pallas_call(kernel, out_shape=out_shape, in_specs=in_vmem(len(operands...  58.6 us
    pallas_call x3, Pallas kernels, call(): pl.pallas_call(kernel, out_shape=out_shape, in_specs=[pl.BlockSpec(memory...  26 us

profile of v4, /device:TPU:0, one launch (start us, length us, event | category | flops | bytes accessed | tf_op | source)
XLA Modules:
  0.0 88.7 jit_solution(5128139886711657144)
XLA Ops:
  1.3 0.7 slice_bitcast_fusion.1
  2.0 0.1 pad_add_fusion
  2.0 0.5 pad.4.list_ref
  2.5 23.5 %shard_map.76 = (bf16[4,2,52,256]{3,2,1,0:T(8,128)(2,1)}, bf16[2,4,52,2048]{3,2,1,0:T(8,128)(2,1)}, bf16[2,4,32,2048]{3,2,1,0:T(8,128)(2,1)}, bf16[4,1,2048]{2,1...) custom-call(bf16[52,2048]{1,0:T(8,128)(2,1)} %bitcast.8, bf16[32,2048]{1,0:T(8,128)(2,1)} %bitcast.9, ...), custom_call_target="tpu_custom_call" | custom-call | tf_op jit(solution)/shard_map/pallas_call | solution.py:526
  26.0 9.8 %shard_map.77.part_ref.rp_ref = f32[4,2,256]{2,1,0:T(2,128)} custom-call(s32[4,1,128]{2,1,0:T(1,128)} %get-tuple-element.16.lists_ref, bf16[4,2,52,256]{3,2,1,0:T(8,128)(2,1)} %get-tuple-element.17.own_ref, bf16[2,4,52,2048]{3,2,1,0:T(8,128)(2,1)} %get-tuple-element.18.next_ref.prev_ref, bf16[4,1,2048]{2,1,0:T(2,128)(2,1)} %get-tuple-element.19.pot_ref), custom_call_target="tpu_custom_call" | custom-call | tf_op jit(solution)/shard_map/pallas_call | solution.py:534
  35.8 13.7 %shard_map.78 = (f32[4,4,2,256]{3,2,1,0:T(2,128)}, f32[4,2,256]{2,1,0:T(2,128)}) custom-call(f32[4,2,256]{2,1,0:T(2,128)} %shard_map.77.part_ref.rp_ref), custom_call_target="tpu_custom_call" | custom-call | tf_op jit(solution)/shard_map/pallas_call | solution.py:526
  49.5 5.5 %shard_map.79 = (f32[4,2,256]{2,1,0:T(2,128)}, f32[8,48,256]{2,1,0:T(8,128)}) custom-call(s32[2,4,1,128]{3,2,1,0:T(1,128)} %get-tuple-element.20.lists_ref, bf16[4,2,52,256]{3,2,1,0:T(8,128)(2,1)} %get-tuple-element.17.own_ref, bf16[2,4,52,2048]{3,2,1,0:T(8,128)(2,1)} %get-tuple-element.18.next_ref.prev_ref, f32[4,4,2,256]{3,2,1,0:T(2,128)} %get-tuple-element.21.rp_ref, ...), custom_call_target="tpu_custom_call" | custom-call | tf_op jit(solution)/shard_map/pallas_call | solution.py:534
  54.9 15.7 %shard_map.80.cp_ref = f32[4,4,2,256]{3,2,1,0:T(2,128)} custom-call(f32[4,2,256]{2,1,0:T(2,128)} %get-tuple-element.23.part_ref), custom_call_target="tpu_custom_call" | custom-call | tf_op jit(solution)/shard_map/pallas_call | solution.py:526
  70.7 10.8 %shard_map.81 = (bf16[4,2,32,256]{3,2,1,0:T(8,128)(2,1)}, f32[1,2048]{1,0:T(1,128)}, f32[1,2048]{1,0:T(1,128)}) custom-call(s32[4,1,128]{2,1,0:T(1,128)} %get-tuple-element.16.lists_ref, bf16[4,2,52,256]{3,2,1,0:T(8,128)(2,1)} %get-tuple-element.17.own_ref, bf16[2,4,52,2048]{3,2,1,0:T(8,128)(2,1)} %get-tuple-element.18.next_ref.prev_ref, ...), custom_call_target="tpu_custom_call" | custom-call | tf_op jit(solution)/shard_map/pallas_call | solution.py:534
  81.5 5.7 %shard_map.82 = bf16[32,2048]{1,0:T(8,128)(2,1)} custom-call(bf16[4,2,32,256]{3,2,1,0:T(8,128)(2,1)} %get-tuple-element.26.smooth_ref), custom_call_target="tpu_custom_call" | custom-call | tf_op jit(solution)/shard_map/pallas_call | solution.py:526
  87.2 1.6 %copy.10 = bf16[1,32,2048]{2,1,0:T(8,128)(2,1)} copy(bf16[1,32,2048]{2,1,0:T(8,128)(2,1)} %bitcast.7) | data formatting | bytes 262144

commit v5 on v4

--- a/solution.py
+++ b/solution.py
@@ -62,17 +62,20 @@
     build[...] = jnp.zeros_like(build)
     ones = jnp.ones((1, TILE), jnp.float32)
 
-    def one(tile, carry):
-        start = pl.multiple_of((tile % tiles_blk) * TILE, TILE)
-        cells = other_ref[tile // tiles_blk, 0:feat, pl.ds(start, TILE)].astype(jnp.float32)
-        build[0:feat, :] = cells
-        build[HALF : HALF + feat, :] = cells
-        bias = split3(bias_of(tile, start, cells))
-        build[HALF - 8 : HALF, :] = rows_of(bias + (ones, ones, ones), TILE)
-        yrec[pl.ds(pl.multiple_of(tile * TILE, TILE), TILE), :] = build[...].T.astype(jnp.bfloat16)
+    def one(block, carry):
+        for step in range(tiles_blk):
+            tile, start, part = block * tiles_blk + step, step * TILE, build.at[step]
+            cells = other_ref[block, 0:feat, start : start + TILE].astype(jnp.float32)
+            part[0:feat, :] = cells
+            part[HALF : HALF + feat, :] = cells
+            bias = split3(bias_of(tile, start, cells))
+            part[HALF - 8 : HALF, :] = rows_of(bias + (ones, ones, ones), TILE)
+        for step in range(tiles_blk):
+            tile = block * tiles_blk + step
+            yrec[pl.ds(pl.multiple_of(tile * TILE, TILE), TILE), :] = build[step].T.astype(jnp.bfloat16)
         return carry
 
-    lax.fori_loop(0, tiles, one, 0)
+    lax.fori_loop(0, tiles // tiles_blk, one, 0)
     lane = lax.broadcasted_iota(jnp.int32, (TILE, 2 * HALF), 1)
     yrec[tiles * TILE : (tiles + 1) * TILE, :] = jnp.where(lane == HALF - 8, NEG, 0.0).astype(
         jnp.bfloat16
@@ -574,7 +577,7 @@
 
     xrec = pltpu.VMEM((held, 2 * HALF, width), bf16)
     yrec = pltpu.VMEM(((tiles + 1) * TILE, 2 * HALF), bf16)
-    build = pltpu.VMEM((2 * HALF, TILE), f32)
+    build = pltpu.VMEM((tiles_blk, 2 * HALF, TILE), f32)
     ext = pltpu.VMEM((tiles + 1, EXT, TILE), bf16)
     stat = pltpu.VMEM((held, 1, width), f32)
     acc = pltpu.VMEM((held, EXT, width), f32)

time: 89 us -> 85 us (0.955)
  Pallas kernels: 84.6 us -> 80.4 us
    pallas_call x3, Pallas kernels: 26 us -> 22.7 us  [call(): pl.pallas_call(kernel, out_shape=out_shape, in_specs=[pl.BlockSpec(memory...]
    pallas_call x4, Pallas kernels: 58.6 us -> 57.6 us  [exchange(): pl.pallas_call(kernel, out_shape=out_shape, in_specs=in_vmem(len(operands...]
where the time goes in v5:
time: 85 us; the launch traced here: 84.5 us
  Pallas kernels  80.4 us (95%)
  local copies, waits for them, and re-layouts  2.76 us (3%)
  between operations  1.31 us (2%)
    pallas_call x4, Pallas kernels, exchange(): pl.pallas_call(kernel, out_shape=out_shape, in_specs=in_vmem(len(operands...  57.6 us
    pallas_call x3, Pallas kernels, call(): pl.pallas_call(kernel, out_shape=out_shape, in_specs=[pl.BlockSpec(memory...  22.7 us

profile of v5, /device:TPU:0, one launch (start us, length us, event | category | flops | bytes accessed | tf_op | source)
XLA Modules:
  0.0 84.5 jit_solution(2566035646748716485)
XLA Ops:
  1.3 0.7 slice_bitcast_fusion.1
  2.0 0.1 pad_add_fusion
  2.0 0.5 pad.4.list_ref
  2.5 23.5 %shard_map.76 = (bf16[4,2,52,256]{3,2,1,0:T(8,128)(2,1)}, bf16[2,4,52,2048]{3,2,1,0:T(8,128)(2,1)}, bf16[2,4,32,2048]{3,2,1,0:T(8,128)(2,1)}, bf16[4,1,2048]{2,1...) custom-call(bf16[52,2048]{1,0:T(8,128)(2,1)} %bitcast.8, bf16[32,2048]{1,0:T(8,128)(2,1)} %bitcast.9, ...), custom_call_target="tpu_custom_call" | custom-call | tf_op jit(solution)/shard_map/pallas_call | solution.py:529
  26.0 8.5 %shard_map.77.part_ref.rp_ref = f32[4,2,256]{2,1,0:T(2,128)} custom-call(s32[4,1,128]{2,1,0:T(1,128)} %get-tuple-element.16.lists_ref, bf16[4,2,52,256]{3,2,1,0:T(8,128)(2,1)} %get-tuple-element.17.own_ref, bf16[2,4,52,2048]{3,2,1,0:T(8,128)(2,1)} %get-tuple-element.18.next_ref.prev_ref, bf16[4,1,2048]{2,1,0:T(2,128)(2,1)} %get-tuple-element.19.pot_ref), custom_call_target="tpu_custom_call" | custom-call | tf_op jit(solution)/shard_map/pallas_call | solution.py:537
  34.6 13.2 %shard_map.78 = (f32[4,4,2,256]{3,2,1,0:T(2,128)}, f32[4,2,256]{2,1,0:T(2,128)}) custom-call(f32[4,2,256]{2,1,0:T(2,128)} %shard_map.77.part_ref.rp_ref), custom_call_target="tpu_custom_call" | custom-call | tf_op jit(solution)/shard_map/pallas_call | solution.py:529
  47.8 4.4 %shard_map.79 = (f32[4,2,256]{2,1,0:T(2,128)}, f32[8,48,256]{2,1,0:T(8,128)}) custom-call(s32[2,4,1,128]{3,2,1,0:T(1,128)} %get-tuple-element.20.lists_ref, bf16[4,2,52,256]{3,2,1,0:T(8,128)(2,1)} %get-tuple-element.17.own_ref, bf16[2,4,52,2048]{3,2,1,0:T(8,128)(2,1)} %get-tuple-element.18.next_ref.prev_ref, f32[4,4,2,256]{3,2,1,0:T(2,128)} %get-tuple-element.21.rp_ref, ...), custom_call_target="tpu_custom_call" | custom-call | tf_op jit(solution)/shard_map/pallas_call | solution.py:537
  52.3 15.2 %shard_map.80.cp_ref = f32[4,4,2,256]{3,2,1,0:T(2,128)} custom-call(f32[4,2,256]{2,1,0:T(2,128)} %get-tuple-element.23.part_ref), custom_call_target="tpu_custom_call" | custom-call | tf_op jit(solution)/shard_map/pallas_call | solution.py:529
  67.5 9.8 %shard_map.81 = (bf16[4,2,32,256]{3,2,1,0:T(8,128)(2,1)}, f32[1,2048]{1,0:T(1,128)}, f32[1,2048]{1,0:T(1,128)}) custom-call(s32[4,1,128]{2,1,0:T(1,128)} %get-tuple-element.16.lists_ref, bf16[4,2,52,256]{3,2,1,0:T(8,128)(2,1)} %get-tuple-element.17.own_ref, bf16[2,4,52,2048]{3,2,1,0:T(8,128)(2,1)} %get-tuple-element.18.next_ref.prev_ref, ...), custom_call_target="tpu_custom_call" | custom-call | tf_op jit(solution)/shard_map/pallas_call | solution.py:537
  77.2 5.7 %shard_map.82 = bf16[32,2048]{1,0:T(8,128)(2,1)} custom-call(bf16[4,2,32,256]{3,2,1,0:T(8,128)(2,1)} %get-tuple-element.26.smooth_ref), custom_call_target="tpu_custom_call" | custom-call | tf_op jit(solution)/shard_map/pallas_call | solution.py:529
  82.9 1.6 %copy.10 = bf16[1,32,2048]{2,1,0:T(8,128)(2,1)} copy(bf16[1,32,2048]{2,1,0:T(8,128)(2,1)} %bitcast.7) | data formatting | bytes 262144

commit v6 on v5

--- a/solution.py
+++ b/solution.py
@@ -55,7 +55,7 @@
         xrec[tile, HALF - 8 : HALF, :] = aux.astype(jnp.bfloat16)
         return carry
 
-    lax.fori_loop(0, tiles, one, 0)
+    lax.fori_loop(0, tiles, one, 0, unroll=4)
 
 
 def other_records(other_ref, yrec, build, feat, tiles_blk, tiles, bias_of):
@@ -92,7 +92,7 @@
         ext[tile, progs:EXT, :] = tail
         return carry
 
-    lax.fori_loop(0, tiles, one, 0)
+    lax.fori_loop(0, tiles, one, 0, unroll=4)
     ext[tiles] = jnp.zeros((EXT, TILE), jnp.bfloat16)
 
 

time: 85 us -> 84.8 us (level)
  no operation moved by 1% of the time
where the time goes in v6:
time: 84.8 us; the launch traced here: 84.3 us
  Pallas kernels  80.2 us (95%)
  local copies, waits for them, and re-layouts  2.76 us (3%)
  between operations  1.31 us (2%)
    pallas_call x4, Pallas kernels, exchange(): pl.pallas_call(kernel, out_shape=out_shape, in_specs=in_vmem(len(operands...  58 us
    pallas_call x3, Pallas kernels, call(): pl.pallas_call(kernel, out_shape=out_shape, in_specs=[pl.BlockSpec(memory...  22.2 us

profile of v6, /device:TPU:0, one launch (start us, length us, event | category | flops | bytes accessed | tf_op | source)
XLA Modules:
  0.0 84.3 jit_solution(3269749239675883068)
XLA Ops:
  1.3 0.7 slice_bitcast_fusion.1
  2.0 0.1 pad_add_fusion
  2.0 0.5 pad.4.list_ref
  2.5 23.5 %shard_map.76 = (bf16[4,2,52,256]{3,2,1,0:T(8,128)(2,1)}, bf16[2,4,52,2048]{3,2,1,0:T(8,128)(2,1)}, bf16[2,4,32,2048]{3,2,1,0:T(8,128)(2,1)}, bf16[4,1,2048]{2,1...) custom-call(bf16[52,2048]{1,0:T(8,128)(2,1)} %bitcast.8, bf16[32,2048]{1,0:T(8,128)(2,1)} %bitcast.9, ...), custom_call_target="tpu_custom_call" | custom-call | tf_op jit(solution)/shard_map/pallas_call | solution.py:529
  26.0 8.5 %shard_map.77.part_ref.rp_ref = f32[4,2,256]{2,1,0:T(2,128)} custom-call(s32[4,1,128]{2,1,0:T(1,128)} %get-tuple-element.16.lists_ref, bf16[4,2,52,256]{3,2,1,0:T(8,128)(2,1)} %get-tuple-element.17.own_ref, bf16[2,4,52,2048]{3,2,1,0:T(8,128)(2,1)} %get-tuple-element.18.next_ref.prev_ref, bf16[4,1,2048]{2,1,0:T(2,128)(2,1)} %get-tuple-element.19.pot_ref), custom_call_target="tpu_custom_call" | custom-call | tf_op jit(solution)/shard_map/pallas_call | solution.py:537
  34.5 13.3 %shard_map.78 = (f32[4,4,2,256]{3,2,1,0:T(2,128)}, f32[4,2,256]{2,1,0:T(2,128)}) custom-call(f32[4,2,256]{2,1,0:T(2,128)} %shard_map.77.part_ref.rp_ref), custom_call_target="tpu_custom_call" | custom-call | tf_op jit(solution)/shard_map/pallas_call | solution.py:529
  47.8 4.3 %shard_map.79 = (f32[4,2,256]{2,1,0:T(2,128)}, f32[8,48,256]{2,1,0:T(8,128)}) custom-call(s32[2,4,1,128]{3,2,1,0:T(1,128)} %get-tuple-element.20.lists_ref, bf16[4,2,52,256]{3,2,1,0:T(8,128)(2,1)} %get-tuple-element.17.own_ref, bf16[2,4,52,2048]{3,2,1,0:T(8,128)(2,1)} %get-tuple-element.18.next_ref.prev_ref, f32[4,4,2,256]{3,2,1,0:T(2,128)} %get-tuple-element.21.rp_ref, ...), custom_call_target="tpu_custom_call" | custom-call | tf_op jit(solution)/shard_map/pallas_call | solution.py:537
  52.1 15.5 %shard_map.80.cp_ref = f32[4,4,2,256]{3,2,1,0:T(2,128)} custom-call(f32[4,2,256]{2,1,0:T(2,128)} %get-tuple-element.23.part_ref), custom_call_target="tpu_custom_call" | custom-call | tf_op jit(solution)/shard_map/pallas_call | solution.py:529
  67.6 9.5 %shard_map.81 = (bf16[4,2,32,256]{3,2,1,0:T(8,128)(2,1)}, f32[1,2048]{1,0:T(1,128)}, f32[1,2048]{1,0:T(1,128)}) custom-call(s32[4,1,128]{2,1,0:T(1,128)} %get-tuple-element.16.lists_ref, bf16[4,2,52,256]{3,2,1,0:T(8,128)(2,1)} %get-tuple-element.17.own_ref, bf16[2,4,52,2048]{3,2,1,0:T(8,128)(2,1)} %get-tuple-element.18.next_ref.prev_ref, ...), custom_call_target="tpu_custom_call" | custom-call | tf_op jit(solution)/shard_map/pallas_call | solution.py:537
  77.0 5.7 %shard_map.82 = bf16[32,2048]{1,0:T(8,128)(2,1)} custom-call(bf16[4,2,32,256]{3,2,1,0:T(8,128)(2,1)} %get-tuple-element.26.smooth_ref), custom_call_target="tpu_custom_call" | custom-call | tf_op jit(solution)/shard_map/pallas_call | solution.py:529
  82.8 1.6 %copy.10 = bf16[1,32,2048]{2,1,0:T(8,128)(2,1)} copy(bf16[1,32,2048]{2,1,0:T(8,128)(2,1)} %bitcast.7) | data formatting | bytes 262144
